TPU v7x, 128 devices: a whole 4x4x4 slice. The times are simulated.
128 devices in a mesh: freq: 16 (over y, x_hi, core), row: 4 (over z), col: 2 (over x_lo).
Axes of the slice: x: 4 (x_hi: 2, x_lo: 2; x = x_hi * 2 + x_lo), y: 4, z: 4, core: 2. Of those that a mesh axis runs over, the one named last changes fastest.
Arguments:
- voltages: bfloat16 [512, 259, 2048], P(('row', 'col', 'freq')), may hold values from -128 to 127, as said below
- tap_table: int32 [4, 2048], replicated, may hold values from -4096 to 4095
Outputs:
- visibility: float32 [1024, 2, 4, 128, 512], P('freq', None, None, 'col', 'row')
Inputs may be any that keep to these rules, and one draw needn't show every extreme that they name: `voltages`: whole numbers.
All inputs are finite; a program needn't handle non-finite values.
Results may differ from a plain program's by a relative error of at most 0.0033.
Values may be sent and summed in bfloat16 or wider, within the bound.
A program may use at most 192 MiB of HBM per device.

v0:
```python
import math

import jax
import jax.numpy as jnp
from jax import lax
from jax.sharding import PartitionSpec as P


def dft_table(length, channels):
    sample = jnp.arange(length, dtype=jnp.int32)
    channel = jnp.arange(channels, dtype=jnp.int32)
    phase = channel[:, None] * sample[None, :] % length
    angle = phase.astype(jnp.float32) * (2.0 * math.pi / length)
    factor = 1.0 / (64.0 * math.sqrt(length))
    return jnp.stack([jnp.cos(angle) * factor, -jnp.sin(angle) * factor], axis=1)


def correlate(column_set, row_block):
    turned = jnp.concatenate([-column_set[:, 1:2], column_set[:, 0:1]], axis=1)
    stacked = jnp.concatenate([column_set, turned], axis=2)
    products = jnp.einsum("cpjt,cpit->cji", stacked, row_block, preferred_element_type=jnp.float32)
    column_count = column_set.shape[2]
    return jnp.stack([products[:, :column_count], products[:, column_count:]], axis=1)


def shards(voltages, tap_table):
    weights = tap_table.astype(jnp.float32) / 4096.0
    spec_count = voltages.shape[1] - tap_table.shape[0] + 1
    filtered = weights[0] * voltages[:, 0:spec_count, :].astype(jnp.float32)
    for tap_index in range(1, tap_table.shape[0]):
        filtered = filtered + weights[tap_index] * voltages[
            :, tap_index : tap_index + spec_count, :
        ].astype(jnp.float32)
    table = dft_table(voltages.shape[2], voltages.shape[2] // 2)
    spectra = jnp.einsum("cpn,isn->cpis", table, filtered, precision=lax.Precision.HIGHEST).astype(
        jnp.bfloat16
    )
    turned_block = lax.all_to_all(spectra, "freq", split_axis=0, concat_axis=2, tiled=True)
    channel_count = turned_block.shape[0]
    group_rows = turned_block.shape[2]
    everyone = lax.all_gather(turned_block, ("row", "col"), axis=2, tiled=True)
    row_size = everyone.shape[2] // lax.axis_size("row")
    row_block = lax.dynamic_slice_in_dim(everyone, lax.axis_index("row") * row_size, row_size, 2)
    grid_view = everyone.reshape(
        channel_count, 2, lax.axis_size("row"), lax.axis_size("col"), group_rows, spec_count
    )
    column_set = lax.dynamic_index_in_dim(grid_view, lax.axis_index("col"), 3, keepdims=False)
    column_set = column_set.reshape(channel_count, 2, lax.axis_size("row") * group_rows, spec_count)
    visibility = correlate(column_set, row_block)
    visibility = visibility / spec_count
    return visibility.reshape(
        channel_count, 2, lax.axis_size("row"), group_rows, row_block.shape[2]
    )


def solution(mesh):
    in_specs = (P(("row", "col", "freq"), None, None), P())
    out_specs = P("freq", None, None, "col", "row")
    return jax.shard_map(shards, mesh=mesh, in_specs=in_specs, out_specs=out_specs, check_vma=False)
```

profile of v0, /device:TPU:2, one launch (start us, length us, event | category | flops | bytes accessed | tf_op | source)
XLA Modules:
  0.0 906.6 jit_solution(9157042138540570160)
XLA Ops:
  6.5 0.0 copy-start.2
  6.5 0.0 all-gather.2.cloned.1.call-start
  6.5 0.0 copy-start.1
  6.5 33.1 %negate_multiply_fusion = (f32[1024,1,2048]{2,0,1:T(8,128)S(1)}, f32[1024,1,2048]{2,0,1:T(8,128)S(1)}) fusion(), kind=kLoop, calls=%fused_computation.23 | loop fusion | flops 35651584 | bytes 16777216 | tf_op jit(solution)/shard_map/mul | solution.py:15
  39.7 0.0 copy-done.2
  39.7 0.0 copy-done.1
  39.7 10.2 %multiply_add_fusion = f32[4,256,2048]{2,0,1:T(4,128)} fusion(bf16[4,259,2048]{2,0,1:T(4,128)(2,1)S(1)} %copy-done.1, f32[2048]{0:T(1024)S(1)} %bitcast.42, f32[2048]{0:T(1024)S(1)} %bitcast.43, f32[2048]{0:T(1024)S(1)} %bitcast.44, f32[2048]{0:T(1024)S(1)} %bitcast.41), kind=kLoop, calls=%fused_computation.22 | loop fusion | flops 23068672 | bytes 25198592 | tf_op jit(solution)/shard_map/add | solution.py:31
  49.9 84.8 %fusion.21 = bf16[1024,2,4,256]{3,0,2,1:T(8,128)(2,1)S(1)} fusion(f32[4,256,2048]{2,0,1:T(4,128)} %multiply_add_fusion, f32[1024,1,2048]{2,0,1:T(8,128)S(1)} %get-tuple-element.13, f32[1024,1,2048]{2,0,1:T(8,128)S(1)} %get-tuple-element.14), kind=kOutput, calls=%fused_computation.29 | convolution fusion | flops 51545899008 | bytes 29360128 | tf_op jit(solution)/shard_map/cpn,isn->cpis/dot_general | solution.py:35
  134.7 3.2 copy.8
  138.0 57.6 %all_to_all.18 = bf16[1024,2,4,256]{3,2,1,0:T(4,128)(2,1)S(1)} all-to-all(bf16[1024,2,4,256]{3,2,1,0:T(4,128)(2,1)S(1)} %copy.8), channel_id=1, replica_groups=mesh['freq'=16,'row'=4,'col'=2] {'freq'}, dimensions={0} | all-to-all | bytes 8388608 | tf_op jit(solution)/shard_map/all_to_all | solution.py:38
  195.6 4.4 copy.22
  200.0 6.9 all_to_all.16
  206.9 0.0 all-gather.2.cloned.1.call-update
  207.0 639.0 %all-gather.2.cloned.1.call-done = bf16[64,2,512,256]{3,2,1,0:T(8,128)(2,1)} async-done(((bf16[64,2,64,256]{3,2,1,0:T(8,128)(2,1)}), bf16[64,2,512,256]{3,2,1,0:T(8,128)(2,1)}) %all-gather.2.cloned.1.call-update) | async-done | bytes 33554448 | tf_op jit(solution)/shard_map/all_gather | solution.py:41
  845.9 8.4 constant_dynamic-slice_fusion
  854.4 0.0 copy-start
  854.4 6.7 slice_negate_fusion
  861.1 4.5 copy-done
  865.6 20.9 %fusion.9 = f32[64,512,128]{2,1,0:T(8,128)} fusion(bf16[64,1,256,256]{3,2,1,0:T(8,128)(2,1)} %get-tuple-element.8, bf16[64,1,256,256]{3,2,1,0:T(8,128)(2,1)} %get-tuple-element.7, bf16[64,2,256,256]{3,2,1,0:T(8,128)(2,1)} %bitcast.35, bf16[64,2,512,256]{3,2,1,0:T(8,128)(2,1)} %all-gather.2.cloned.1.call-done, s32[]{:T(128)S(6)} %select_n.29), kind=kOutput, calls=%fused_computation.14 | convolution fusion | flops 4395630592 | bytes 58720260 | tf_op jit(solution)/shard_map/cpjt,cpit->cji/dot_general | solution.py:21
  886.5 6.5 fusion.27
  892.9 6.4 maximum_multiply_fusion
  (2 shorter events, 0.0 us)
Async XLA Ops:
  6.5 33.1 %copy-start.2 = (s32[4,2048]{1,0:T(4,128)S(1)}, s32[4,2048]{1,0:T(4,128)}, u32[]{:S(2)}) copy-start(s32[4,2048]{1,0:T(4,128)} %param.3) | copy-start | bytes 98308
  6.5 839.4 %all-gather.2.cloned.1.call-start = ((), (), s32[]{:S(2)}) async-start(), calls=%async_computation.1 | async-start | bytes 37748736 | tf_op jit(solution)/shard_map/all_gather | solution.py:41
  6.5 33.2 %copy-start.1 = (bf16[4,259,2048]{2,0,1:T(4,128)(2,1)S(1)}, bf16[4,259,2048]{2,0,1:T(4,128)(2,1)}, u32[]{:S(2)}) copy-start(bf16[4,259,2048]{2,0,1:T(4,128)(2,1)} %param.2) | copy-start | bytes 12730372
  854.4 11.2 %copy-start = (bf16[64,2,4,1,64,256]{5,4,3,2,1,0:T(8,128)(2,1)}, bf16[64,2,4,1,64,256]{5,4,3,2,1,0:T(8,128)(2,1)S(1)}, u32[]{:S(2)}) copy-start(bf16[64,2,4,1,64,256]{5,4,3,2,1,0:T(8,128)(2,1)S(1)} %constant_dynamic-slice_fusion) | copy-start | bytes 50331652
Sparse Core Ops, SparseCore 0:
  207.1 638.8 all-gather.1
where the time goes:
time: 916 us; the launch traced here: 907 us
  waiting for transfers between devices  639 us (70%)
  matrix products  106 us (12%)
  blocking collectives  57.6 us (6%)
  other arithmetic  56.4 us (6%)
  local copies, waits for them, and re-layouts  34 us (4%)
  between operations  13.9 us (2%)
    all_gather x1, waiting for transfers between devices, shards(): everyone = lax.all_gather(turned_block, ('row', 'col'), axis=2, tiled=True)  639 us
    dot_general x1, matrix products, shards(): jnp.einsum('cpn,isn->cpis', table, filtered, precision=lax.Precision.HIGH...  84.8 us
    all_to_all x1, blocking collectives, shards(): lax.all_to_all(spectra, 'freq', split_axis=0, concat_axis=2, tiled=True)  57.6 us
    mul x1, other arithmetic, dft_table(): -jnp.sin(angle) * factor  33.1 us
    dot_general x1, matrix products, correlate(): jnp.einsum('cpjt,cpit->cji', stacked, row_block, preferred_element_type=j...  20.9 us
  transfers between devices with their start and end apart: 1, of which 1 were waited for; matrix products, arithmetic and copies ran while one was open for 0% of the time, Pallas kernels for 0%

commit v1 on v0

v1 whole, which is shorter than its diff:
```python
import functools
import math

import jax
import jax.numpy as jnp
import ml_dtypes
import numpy as np
from jax import lax
from jax.experimental import pallas as pl
from jax.experimental.pallas import tpu as pltpu
from jax.sharding import PartitionSpec as P

NFFT = 2048
HALF = NFFT // 2
TAPS = 4
SPEC = 256
CHAN = 1024
GROUPS = 16
LOCAL_CHAN = CHAN // GROUPS
CHUNKS = 4
CHUNK_CHAN = LOCAL_CHAN // CHUNKS
FOLD_CHAN = CHUNK_CHAN // 2
TARGETS = 8
ROWS = 2 * TARGETS * FOLD_CHAN
F32 = jnp.float32
BF16 = jnp.bfloat16
MESH = pl.DeviceIdType.MESH


def dft_tables():
    core, chunk, parity, part, target, index = np.meshgrid(
        np.arange(2), np.arange(CHUNKS), np.arange(2), np.arange(2), np.arange(TARGETS), np.arange(FOLD_CHAN),
        indexing="ij",
    )
    channel = (target * 2 + core) * LOCAL_CHAN + chunk * CHUNK_CHAN + 2 * index + parity
    phase = (channel[..., None] * np.arange(HALF)) % NFFT
    angle = phase * (2.0 * np.pi / NFFT)
    cosine = np.where(phase % (NFFT // 2) == NFFT // 4, 0.0, np.cos(angle))
    sine = np.where(phase % (NFFT // 2) == 0, 0.0, np.sin(angle))
    values = np.where(part[..., None] == 0, cosine, -sine) / (64.0 * math.sqrt(NFFT) * 4096.0)
    high = values.astype(ml_dtypes.bfloat16)
    low = (values - high.astype(np.float64)).astype(ml_dtypes.bfloat16)
    shape = (2, CHUNKS, 2, ROWS, HALF)
    return np.concatenate([high.reshape(shape), low.reshape(shape)], axis=3)


def spectrum_kernel(core_ref, own_ref, other_ref, weight_ref, table_ref, out_ref, frames, folded, turned):
    core = core_ref[0]

    @pl.when(pl.program_id(0) == 0)
    def _():
        for source, first in ((own_ref, 0), (other_ref, 4)):

            @pl.loop(0, 4 * (HALF // 128))
            def _(step):
                row = step // (HALF // 128)
                low = pl.multiple_of((step % (HALF // 128)) * 128, 128)
                high = pl.multiple_of(low + HALF, 128)
                count = SPEC + TAPS - 1
                frames[0, 0:count, :] = source[row, :, pl.ds(low, 128)].astype(F32)
                frames[1, 0:count, :] = source[row, :, pl.ds(high, 128)].astype(F32)
                for start in range(0, SPEC, 64):
                    halves = []
                    for half, column in ((0, low), (1, high)):
                        total = None
                        for tap in range(TAPS):
                            weight = weight_ref[pl.ds(tap, 1), pl.ds(column, 128)]
                            term = weight * frames[half, start + tap : start + tap + 64, :]
                            total = term if total is None else total + term
                        halves.append(total)
                    for parity, value in ((0, halves[0] + halves[1]), (1, halves[0] - halves[1])):
                        top = value.astype(BF16)
                        rest = (value - top.astype(F32)).astype(BF16)
                        folded[parity, 0, first + row, start : start + 64, pl.ds(low, 128)] = top
                        folded[parity, 1, first + row, start : start + 64, pl.ds(low, 128)] = rest

    contract = (((1,), (1,)), ((), ()))

    @pl.loop(0, 8)
    def _(slot):
        row = lax.rem(slot + 4 * core, 8)
        for parity in range(2):
            top = folded[parity, 0, slot]
            both = lax.dot_general(table_ref[0, 0, parity], top, contract, preferred_element_type=F32)
            rest = lax.dot_general(
                table_ref[0, 0, parity, :ROWS], folded[parity, 1, slot], contract, preferred_element_type=F32
            )
            value = both[:ROWS] + both[ROWS:] + rest
            for part in range(2):
                for target in range(TARGETS):
                    first = (part * TARGETS + target) * FOLD_CHAN
                    start = target * (CHUNK_CHAN * 16) + parity * 16 + part * 8 + row
                    for half in range(2):
                        turned[half, pl.ds(start, FOLD_CHAN, stride=32), :] = value[
                            first : first + FOLD_CHAN, half * 128 : half * 128 + 128
                        ]

    block = CHUNK_CHAN * 16

    @pl.loop(0, TARGETS)
    def _(target):
        for half in range(2):
            rows = turned[half, pl.ds(pl.multiple_of(target * block, block), block), :]
            out_ref[0, target, :, :, half * 128 : half * 128 + 128] = rows.reshape(2 * CHUNK_CHAN, 8, 128).astype(BF16)


def spectra(own, other, weights, table, core):
    whole = lambda shape: pl.BlockSpec(shape, lambda k, c: (0,) * len(shape))
    return pl.pallas_call(
        spectrum_kernel,
        grid_spec=pltpu.PrefetchScalarGridSpec(
            num_scalar_prefetch=1,
            grid=(CHUNKS,),
            in_specs=[
                whole(own.shape),
                whole(other.shape),
                whole(weights.shape),
                pl.BlockSpec((1, 1, 2, 2 * ROWS, HALF), lambda k, c: (c[0], k, 0, 0, 0)),
            ],
            out_specs=pl.BlockSpec((1, TARGETS, 2 * CHUNK_CHAN, 8, SPEC), lambda k, c: (k, 0, 0, 0, 0)),
            scratch_shapes=[
                pltpu.VMEM((2, 272, 128), F32),
                pltpu.VMEM((2, 2, 8, SPEC, HALF), BF16),
                pltpu.VMEM((2, TARGETS * CHUNK_CHAN * 16, 128), F32),
            ],
        ),
        out_shape=jax.ShapeDtypeStruct((CHUNKS, TARGETS, 2 * CHUNK_CHAN, 8, SPEC), BF16),
        compiler_params=pltpu.CompilerParams(vmem_limit_bytes=56 << 20),
        name="spectra",
    )(core, own, other, weights, table)


def exchange_kernel(
    spec_ref, rows, planes, local_sem, first_send, first_recv, pair_send, pair_recv, ring_send, ring_recv, pass_send, pass_recv
):
    freq, z, xl = lax.axis_index("freq"), lax.axis_index("row"), lax.axis_index("col")
    core = lax.rem(freq, 2)
    xh = lax.rem(freq // 2, 2)
    y = freq // 4
    up, down = lax.rem(z + 1, 4), lax.rem(z + 3, 4)

    def device(to_y, to_xh, to_z, to_xl):
        return {"freq": (to_y * 2 + to_xh) * 2 + core, "row": to_z, "col": to_xl}

    partner = device(y, xh, z, 1 - xl)
    above, below = device(y, xh, up, xl), device(y, xh, down, xl)

    barrier = pltpu.get_barrier_semaphore()
    others = [device(lax.rem(y + step, 4), xh, z, xl) for step in range(1, 4)]
    others += [device(lax.rem(y + step, 4), 1 - xh, z, 1 - xl) for step in range(4)]
    others += [partner, above, below]
    for other in others:
        pl.semaphore_signal(barrier, inc=1, device_id=other, device_id_type=MESH)
    pl.semaphore_wait(barrier, len(others))

    def remote(source, target, send, recv, where):
        return pltpu.make_async_remote_copy(
            src_ref=source, dst_ref=target, send_sem=send, recv_sem=recv, device_id=where, device_id_type=MESH
        )

    def first(k, step, flip):
        to_y, to_xh, to_xl = lax.rem(y + step, 4), (1 - xh if flip else xh), (1 - xl if flip else xl)
        index = flip * 4 + step
        return remote(
            spec_ref.at[k, to_y * 2 + to_xh],
            rows.at[k, :, xl, y, xh],
            first_send.at[k, index],
            first_recv.at[k, index],
            device(to_y, to_xh, z, to_xl),
        )

    def first_arrival(k, step, flip):
        from_y, from_xh, from_xl = lax.rem(y + 4 - step, 4), (1 - xh if flip else xh), (1 - xl if flip else xl)
        index = flip * 4 + step
        place = rows.at[k, :, from_xl, from_y, from_xh]
        return remote(place, place, first_send.at[k, index], first_recv.at[k, index], device(from_y, from_xh, z, from_xl))

    def local(k):
        return pltpu.make_async_copy(spec_ref.at[k, y * 2 + xh], rows.at[k, :, xl, y, xh], local_sem.at[k])

    def block(k, part, mine):
        side = xl if part == 0 else 1 - xl
        if not mine:
            side = 1 - side
        return rows.at[k, :, side, :, xh if part == 0 else 1 - xh]

    def pair(k, part, mine=True):
        place = block(k, part, mine)
        return remote(place, place, pair_send.at[k, part], pair_recv.at[k, part], partner)

    def ring(k, part, way):
        column = xh if part == 0 else 1 - xh
        return remote(
            rows.at[k, :, xl, :, column],
            planes.at[way, k, :, :, column],
            ring_send.at[k, part, way],
            ring_recv.at[k, part, way],
            above if way == 0 else below,
        )

    def onward(k, part):
        column = xh if part == 0 else 1 - xh
        return remote(
            planes.at[part, k, :, :, column],
            planes.at[2, k, :, :, column],
            pass_send.at[k, part],
            pass_recv.at[k, part],
            above if part == 0 else below,
        )

    for k in range(CHUNKS):
        local(k).start()
        for step in range(1, 4):
            first(k, step, 0).start()
        for step in range(4):
            first(k, step, 1).start()

    for turn in range(CHUNKS + 2):
        k = turn
        if k < CHUNKS:
            local(k).wait()
            for step in range(1, 4):
                first_arrival(k, step, 0).wait_recv()
            for way in range(2):
                ring(k, 0, way).start()
            pair(k, 0).start()
            for step in range(4):
                first_arrival(k, step, 1).wait_recv()
            pair(k, 1).start()
        k = turn - 1
        if 0 <= k < CHUNKS:
            pair(k, 1, False).wait_recv()
            for way in range(2):
                ring(k, 1, way).start()
        k = turn - 2
        if 0 <= k < CHUNKS:
            for part in range(2):
                ring(k, part, part).wait_recv()
                onward(k, part).start()

    for k in range(CHUNKS):
        pair(k, 0, False).wait_recv()
        for part in range(2):
            ring(k, part, 1 - part).wait_recv()
            onward(k, part).wait_recv()
    for k in range(CHUNKS):
        for step in range(1, 4):
            first(k, step, 0).wait_send()
        for step in range(4):
            first(k, step, 1).wait_send()
        for part in range(2):
            pair(k, part).wait_send()
            for way in range(2):
                ring(k, part, way).wait_send()
            onward(k, part).wait_send()


def exchange(spec):
    any_space = pl.BlockSpec(memory_space=pl.ANY)
    dma = pltpu.SemaphoreType.DMA
    return pl.pallas_call(
        exchange_kernel,
        in_specs=[any_space],
        out_specs=[any_space, any_space],
        out_shape=[
            jax.ShapeDtypeStruct((CHUNKS, 2 * CHUNK_CHAN, 2, 4, 2, 8, SPEC), BF16),
            jax.ShapeDtypeStruct((3, CHUNKS, 2 * CHUNK_CHAN, 4, 2, 8, SPEC), BF16),
        ],
        scratch_shapes=[
            dma((CHUNKS,)),
            dma((CHUNKS, 8)),
            dma((CHUNKS, 8)),
            dma((CHUNKS, 2)),
            dma((CHUNKS, 2)),
            dma((CHUNKS, 2, 2)),
            dma((CHUNKS, 2, 2)),
            dma((CHUNKS, 2)),
            dma((CHUNKS, 2)),
        ],
        compiler_params=pltpu.CompilerParams(collective_id=0, has_side_effects=True),
        name="exchange",
    )(spec)


def correlate_kernel(step_chan, place_ref, rows_ref, planes_ref, out_ref):
    z, xl = place_ref[0], place_ref[1]
    for c in range(step_chan):
        real, imag = rows_ref[c, 0], rows_ref[c, 1]
        weights = jnp.concatenate(
            [jnp.concatenate([real, imag], axis=1), jnp.concatenate([imag, -real], axis=1)], axis=0
        )
        start = pl.multiple_of(xl * 64, 64)
        pieces = [jnp.concatenate([rows_ref[c, 0, pl.ds(start, 64)], rows_ref[c, 1, pl.ds(start, 64)]], axis=1)]
        for slot in range(3):
            pieces.append(jnp.concatenate([planes_ref[slot, c, 0], planes_ref[slot, c, 1]], axis=1))
        for piece, shift in zip(pieces, (0, 3, 1, 2)):
            value = lax.dot_general(piece, weights, (((1,), (1,)), ((), ())), preferred_element_type=F32) * (1.0 / SPEC)
            plane = lax.rem(z + shift, 4)
            out_ref[c, 0, plane] = value[:, :128]
            out_ref[c, 1, plane] = value[:, 128:]


def correlate(rows, planes, place):
    step_chan = 4
    return pl.pallas_call(
        functools.partial(correlate_kernel, step_chan),
        grid_spec=pltpu.PrefetchScalarGridSpec(
            num_scalar_prefetch=1,
            grid=(LOCAL_CHAN // step_chan,),
            in_specs=[
                pl.BlockSpec((step_chan, 2, 128, SPEC), lambda g, p: (g, 0, 0, 0)),
                pl.BlockSpec((3, step_chan, 2, 64, SPEC), lambda g, p: (0, g, 0, 0, 0)),
            ],
            out_specs=pl.BlockSpec((step_chan, 2, 4, 64, 128), lambda g, p: (g, 0, 0, 0, 0)),
        ),
        out_shape=jax.ShapeDtypeStruct((LOCAL_CHAN, 2, 4, 64, 128), F32),
        compiler_params=pltpu.CompilerParams(vmem_limit_bytes=40 << 20),
        name="correlate",
    )(place, rows, planes)


def shards(table, voltages, tap_table):
    freq, z, xl = lax.axis_index("freq"), lax.axis_index("row"), lax.axis_index("col")
    weights = tap_table.astype(F32)
    other = lax.ppermute(voltages, "freq", [(f, f ^ 1) for f in range(GROUPS)])
    core = (freq % 2).astype(jnp.int32).reshape(1)
    spec = spectra(voltages, other, weights, table, core)
    rows, planes = exchange(spec)
    rows = rows.reshape(LOCAL_CHAN, 2, 128, SPEC)
    planes = planes.reshape(3, LOCAL_CHAN, 2, 64, SPEC)
    return correlate(rows, planes, jnp.stack([z, xl]).astype(jnp.int32))


def solution(mesh):
    table = dft_tables()

    def run(voltages, tap_table):
        return jax.shard_map(
            shards,
            mesh=mesh,
            in_specs=(P(), P(("row", "col", "freq"), None, None), P()),
            out_specs=P("freq", None, None, "col", "row"),
            check_vma=False,
        )(jnp.asarray(table), voltages, tap_table)

    return run
```

time: 916 us -> 250 us (0.27)
  waiting for transfers between devices: 639 us -> 0.27 us
  Pallas kernels: 0 us -> 231 us
  matrix products: 106 us -> 0 us
  blocking collectives: 57.6 us -> 0 us
  other arithmetic: 56.4 us -> 0.7 us
  local copies, waits for them, and re-layouts: 34 us -> 16.5 us
  between operations: 13.9 us -> 0.02 us
    all_gather x1 -> x0, waiting for transfers between devices: 639 us -> none  [shards(): everyone = lax.all_gather(turned_block, ('row', 'col'), axis=2, tiled=True)]
    pallas_call x0 -> x3, Pallas kernels: none -> 231 us  [the longest x1 160 us: exchange(): pl.pallas_call(exchange_kernel, in_specs=[any_space], out_specs=[any_spac...]
    dot_general x2 -> x0, matrix products: 106 us -> none  [the longest x1 84.8 us: shards(): jnp.einsum('cpn,isn->cpis', table, filtered, precision=lax.Precision.HIGH...]
    all_to_all x1 -> x0, blocking collectives: 57.6 us -> none  [shards(): lax.all_to_all(spectra, 'freq', split_axis=0, concat_axis=2, tiled=True)]
    mul x1 -> x0, other arithmetic: 33.1 us -> none  [dft_table(): -jnp.sin(angle) * factor]
    all_to_all x2 -> x0, local copies, waits for them, and re-layouts: 11.3 us -> none  [shards(): lax.all_to_all(spectra, 'freq', split_axis=0, concat_axis=2, tiled=True)]
    add x1 -> x0, other arithmetic: 10.2 us -> none  [shards(): filtered + weights[tap_index] * voltages[:, tap_index:tap_index + spec_co...]
  transfers between devices with their start and end apart: 1 -> 1, of which waited for: 1 -> 1; matrix products, arithmetic and copies ran while one was open for 0% -> 3% of each run, Pallas kernels for 0% -> 0%
where the time goes in v1:
time: 250 us; the launch traced here: 249 us
  Pallas kernels  231 us (92%)
  local copies, waits for them, and re-layouts  16.5 us (7%)
    pallas_call x1, Pallas kernels, exchange(): pl.pallas_call(exchange_kernel, in_specs=[any_space], out_specs=[any_spac...  160 us
    pallas_call x1, Pallas kernels, spectra(): pl.pallas_call(spectrum_kernel, grid_spec=pltpu.PrefetchScalarGridSpec(nu...  45.8 us
    pallas_call x1, Pallas kernels, correlate(): pl.pallas_call(functools.partial(correlate_kernel, step_chan), grid_spec=...  25.9 us
    unnamed x5, local copies, waits for them, and re-layouts  9.97 us
    ppermute x1, local copies, waits for them, and re-layouts, shards(): other = lax.ppermute(voltages, 'freq', [(f, f ^ 1) for f in range(GROUPS)])  6.52 us
  transfers between devices with their start and end apart: 1, of which 1 were waited for; matrix products, arithmetic and copies ran while one was open for 3% of the time, Pallas kernels for 0%

profile of v1, /device:TPU:2, one launch (start us, length us, event | category | flops | bytes accessed | tf_op | source)
XLA Modules:
  0.0 248.9 jit_solution(10326923244738991499)
XLA Ops:
  0.0 0.0 copy-start.1
  0.0 0.0 collective-permute-start
  0.0 6.6 %copy.6.own_ref = bf16[4,259,2048]{2,1,0:T(8,128)(2,1)} copy(bf16[4,259,2048]{2,0,1:T(4,128)(2,1)} %param.3) | data formatting | bytes 8486912 | tf_op args[0]
  6.6 0.0 copy-done.1
  6.6 0.6 convert_element_type.3.weight_ref
  7.2 0.1 pad_add_fusion.place_ref
  7.3 0.3 collective-permute-done
  7.6 6.5 %copy.7.other_ref = bf16[4,259,2048]{2,1,0:T(8,128)(2,1)} copy(bf16[4,259,2048]{2,0,1:T(4,128)(2,1)} %collective-permute-done) | data formatting | bytes 8486912 | tf_op jit(solution)/shard_map/ppermute | solution.py:325
  14.1 45.8 %spectra.1.spec_ref = bf16[4,8,32,8,256]{4,3,2,1,0:T(8,128)(2,1)} custom-call(s32[1]{0:T(128)} %bitcast.2.core_ref, bf16[4,259,2048]{2,1,0:T(8,128)(2,1)} %copy.6.own_ref, bf16[4,259,2048]{2,1,0:T(8,128)(2,1)} %copy.7.other_ref, f32[4,2048]{1,0:T(4,128)} %convert_element_type.3.weight_ref, bf16[2,4,2,256,1024]{4,3,2,1,0:T(8,128)(2,1)} %constant.28.clone.table_ref), custom_call_target="tpu_custom_call" | custom-call | tf_op jit(solution)/shard_map/spectra/pallas_call | solution.py:109
  59.9 159.6 %exchange.1 = (bf16[4,32,2,4,2,8,256]{6,5,4,3,2,1,0:T(8,128)(2,1)}, bf16[3,4,32,4,2,8,256]{6,5,4,3,2,1,0:T(8,128)(2,1)}) custom-call(bf16[4,8,32,8,256]{4,3,2,1,0:T(8,128)(2,1)} %spectra.1.spec_ref), custom_call_target="tpu_custom_call" | custom-call | tf_op jit(solution)/shard_map/exchange/pallas_call | solution.py:261
  219.5 0.0 copy-start
  219.5 3.4 %copy-done = bf16[4,32,2,4,2,8,256]{6,5,4,3,2,1,0:T(8,128)(2,1)S(1)} copy-done((bf16[4,32,2,4,2,8,256]{6,5,4,3,2,1,0:T(8,128)(2,1)S(1)}, bf16[4,32,2,4,2,8,256]{6,5,4,3,2,1,0:T(8,128)(2,1)}, u32[]{:S(2)}) %copy-start) | copy-done | bytes 8388632
  222.9 25.9 %correlate.1 = f32[64,2,4,64,128]{4,3,2,1,0:T(8,128)} custom-call(s32[2]{0:T(128)S(1)} %pad_add_fusion.place_ref, bf16[64,2,128,256]{3,2,1,0:T(8,128)(2,1)S(1)} %bitcast.5, bf16[3,64,2,64,256]{4,3,2,1,0:T(8,128)(2,1)} %bitcast.6), custom_call_target="tpu_custom_call" | custom-call | tf_op jit(solution)/shard_map/correlate/pallas_call | solution.py:305
Async XLA Ops:
  0.0 6.6 %copy-start.1 = (s32[4,2048]{1,0:T(4,128)S(1)}, s32[4,2048]{1,0:T(4,128)}, u32[]{:S(2)}) copy-start(s32[4,2048]{1,0:T(4,128)} %param.4) | copy-start | bytes 98308
  0.0 7.6 %collective-permute-start = (bf16[4,259,2048]{2,0,1:T(4,128)(2,1)}, bf16[4,259,2048]{2,0,1:T(4,128)(2,1)}, u32[]{:S(2)}, u32[]{:S(2)}) collective-permute-start(bf16[4,259,2048]{2,0,1:T(4,128)(2,1)} %param.3), channel_id=1, source_target_pairs={{0,8},{8,0},{16,24},{24,16},{32,40},{40,32},{48,56},{56,48},{64,72... | collective-permute-start | bytes 12730376 | tf_op jit(solution)/shard_map/ppermute | solution.py:325
  219.5 3.4 %copy-start = (bf16[4,32,2,4,2,8,256]{6,5,4,3,2,1,0:T(8,128)(2,1)S(1)}, bf16[4,32,2,4,2,8,256]{6,5,4,3,2,1,0:T(8,128)(2,1)}, u32[]{:S(2)}) copy-start(bf16[4,32,2,4,2,8,256]{6,5,4,3,2,1,0:T(8,128)(2,1)} %get-tuple-element.7) | copy-start | bytes 25165828

commit v2 on v0

v2 whole, which is shorter than its diff:
```python
import math

import jax
import jax.numpy as jnp
import ml_dtypes
import numpy as np
from jax import lax
from jax.experimental import pallas as pl
from jax.experimental.pallas import tpu as pltpu
from jax.sharding import PartitionSpec as P

NFFT = 2048
HALF = NFFT // 2
TAPS = 4
SPEC = 256
CHAN = 1024
GROUPS = 16
LOCAL_CHAN = CHAN // GROUPS
CHUNKS = 4
CHUNK_CHAN = LOCAL_CHAN // CHUNKS
FOLD_CHAN = CHUNK_CHAN // 2
TARGETS = 8
ROWS = 2 * TARGETS * FOLD_CHAN
HALF_SPEC = SPEC // 2
STEPS = 2 * CHUNKS
STEP_CHAN = 4
F32 = jnp.float32
BF16 = jnp.bfloat16
MESH = pl.DeviceIdType.MESH


def dft_tables():
    core, chunk, parity, part, target, index = np.meshgrid(
        np.arange(2), np.arange(CHUNKS), np.arange(2), np.arange(2), np.arange(TARGETS), np.arange(FOLD_CHAN),
        indexing="ij",
    )
    channel = (target * 2 + core) * LOCAL_CHAN + chunk * CHUNK_CHAN + 2 * index + parity
    phase = (channel[..., None] * np.arange(HALF)) % NFFT
    angle = phase * (2.0 * np.pi / NFFT)
    cosine = np.where(phase % (NFFT // 2) == NFFT // 4, 0.0, np.cos(angle))
    sine = np.where(phase % (NFFT // 2) == 0, 0.0, np.sin(angle))
    values = np.where(part[..., None] == 0, cosine, -sine) / (64.0 * math.sqrt(NFFT) * 4096.0)
    high = values.astype(ml_dtypes.bfloat16)
    low = (values - high.astype(np.float64)).astype(ml_dtypes.bfloat16)
    shape = (2, CHUNKS, 2, ROWS, HALF)
    return np.concatenate([high.reshape(shape), low.reshape(shape)], axis=3)


def filter_half(half, source, first, weight_ref, frames, folded):
    count = HALF_SPEC + TAPS - 1

    @pl.loop(0, HALF // 128)
    def _(step):
        low = pl.multiple_of(step * 128, 128)
        columns = (low, pl.multiple_of(low + HALF, 128))
        for side in range(2):
            block = source[pl.ds(half * HALF_SPEC, count), :, pl.ds(columns[side], 128)]
            frames[side, 0 : 4 * count, :] = block.astype(F32).reshape(4 * count, 128)
        for row in range(4):
            slot = first + row
            for start in range(0, HALF_SPEC, 64):
                sides = []
                for side in range(2):
                    total = None
                    for tap in range(TAPS):
                        weight = weight_ref[pl.ds(tap, 1), pl.ds(columns[side], 128)]
                        term = weight * frames[side, pl.ds((start + tap) * 4 + row, 64, stride=4), :]
                        total = term if total is None else total + term
                    sides.append(total)
                place = (slot % 2) * HALF_SPEC + start
                for parity, value in ((0, sides[0] + sides[1]), (1, sides[0] - sides[1])):
                    top = value.astype(BF16)
                    rest = (value - top.astype(F32)).astype(BF16)
                    folded[parity, 0, half, slot // 2, place : place + 64, pl.ds(low, 128)] = top
                    folded[parity, 1, half, slot // 2, place : place + 64, pl.ds(low, 128)] = rest


def transform_chunk(half, quarter, core, table_ref, folded, turned, write):
    contract = (((1,), (1,)), ((), ()))

    @pl.loop(0, 4)
    def _(duo):
        for parity in range(2):
            top = folded[parity, 0, half, duo]
            both = lax.dot_general(table_ref[quarter, parity], top, contract, preferred_element_type=F32)
            rest = lax.dot_general(
                table_ref[quarter, parity, :ROWS], folded[parity, 1, half, duo], contract, preferred_element_type=F32
            )
            value = both[:ROWS] + both[ROWS:] + rest
            for sub in range(2):
                row = lax.rem(2 * duo + sub + 4 * core, 8)
                for part in range(2):
                    turned[pl.ds(parity * 16 + part * 8 + row, ROWS // 2, stride=32), :] = value[
                        part * (ROWS // 2) : (part + 1) * (ROWS // 2), sub * 128 : sub * 128 + 128
                    ]

    block = CHUNK_CHAN * 16

    @pl.loop(0, TARGETS)
    def _(target):
        rows = turned[pl.ds(pl.multiple_of(target * block, block), block), :]
        write(target, rows.reshape(2 * CHUNK_CHAN, 8, 128).astype(BF16))


def exchange_kernel(
    own_ref, weight_ref, table_hbm, rows, planes,
    own, other, table, frames, folded, turned, made,
    load_sem, table_sem, core_send, core_recv,
    local_sem, first_send, first_recv, pair_send, pair_recv, ring_send, ring_recv, pass_send, pass_recv,
):
    freq, z, xl = lax.axis_index("freq"), lax.axis_index("row"), lax.axis_index("col")
    core = lax.rem(freq, 2)
    xh = lax.rem(freq // 2, 2)
    y = freq // 4
    up, down = lax.rem(z + 1, 4), lax.rem(z + 3, 4)
    pieces = (pl.ds(0, HALF_SPEC + TAPS - 1), pl.ds(HALF_SPEC + TAPS - 1, HALF_SPEC))

    def load(part):
        return pltpu.make_async_copy(own_ref.at[pieces[part]], own.at[pieces[part]], load_sem.at[part])

    def load_table(quarter):
        return pltpu.make_async_copy(table_hbm.at[core, quarter], table.at[quarter], table_sem.at[quarter])

    load(0).start()
    for quarter in range(CHUNKS):
        load_table(quarter).start()
    load(1).start()

    def device(to_y, to_xh, to_z, to_xl, to_core=core):
        return {"freq": (to_y * 2 + to_xh) * 2 + to_core, "row": to_z, "col": to_xl}

    sibling = device(y, xh, z, xl, 1 - core)
    partner = device(y, xh, z, 1 - xl)
    above, below = device(y, xh, up, xl), device(y, xh, down, xl)

    barrier = pltpu.get_barrier_semaphore()
    others = [sibling]
    others += [device(lax.rem(y + step, 4), xh, z, xl) for step in range(1, 4)]
    others += [device(lax.rem(y + step, 4), 1 - xh, z, 1 - xl) for step in range(4)]
    others += [partner, above, below]
    for one in others:
        pl.semaphore_signal(barrier, inc=1, device_id=one, device_id_type=MESH)
    pl.semaphore_wait(barrier, len(others))

    def remote(source, target, send, recv, where):
        return pltpu.make_async_remote_copy(
            src_ref=source, dst_ref=target, send_sem=send, recv_sem=recv, device_id=where, device_id_type=MESH
        )

    def swap(part):
        return remote(
            own_ref.at[pieces[part]], other.at[pieces[part]], core_send.at[part], core_recv.at[part], sibling
        )

    for part in range(2):
        swap(part).start()

    def spot(t):
        return lax.rem(t, CHUNKS), pl.ds(pl.multiple_of((t // CHUNKS) * HALF_SPEC, HALF_SPEC), HALF_SPEC)

    def home(t, side, from_y, from_xh):
        k, lanes = spot(t)
        return rows.at[k, :, side, from_y, from_xh, :, lanes]

    def first(t, step, flip):
        to_y, to_xh, to_xl = lax.rem(y + step, 4), (1 - xh if flip else xh), (1 - xl if flip else xl)
        index = flip * 4 + step
        return remote(
            made.at[t, to_y * 2 + to_xh], home(t, xl, y, xh),
            first_send.at[t, index], first_recv.at[t, index], device(to_y, to_xh, z, to_xl),
        )

    def first_arrival(t, step, flip):
        from_y, from_xh, from_xl = lax.rem(y + 4 - step, 4), (1 - xh if flip else xh), (1 - xl if flip else xl)
        index = flip * 4 + step
        place = home(t, from_xl, from_y, from_xh)
        return remote(
            place, place, first_send.at[t, index], first_recv.at[t, index], device(from_y, from_xh, z, from_xl)
        )

    def local(t):
        return pltpu.make_async_copy(made.at[t, y * 2 + xh], home(t, xl, y, xh), local_sem.at[t])

    def pair(t, part, mine=True):
        k, lanes = spot(t)
        side = xl if (part == 0) == mine else 1 - xl
        place = rows.at[k, :, side, :, xh if part == 0 else 1 - xh, :, lanes]
        return remote(place, place, pair_send.at[t, part], pair_recv.at[t, part], partner)

    def ring(t, part, way):
        k, lanes = spot(t)
        column = xh if part == 0 else 1 - xh
        return remote(
            rows.at[k, :, xl, :, column, :, lanes], planes.at[way, k, :, :, column, :, lanes],
            ring_send.at[t, part, way], ring_recv.at[t, part, way], above if way == 0 else below,
        )

    def onward(t, part):
        k, lanes = spot(t)
        column = xh if part == 0 else 1 - xh
        return remote(
            planes.at[part, k, :, :, column, :, lanes], planes.at[2, k, :, :, column, :, lanes],
            pass_send.at[t, part], pass_recv.at[t, part], above if part == 0 else below,
        )

    def fold(half):
        load(half).wait()
        filter_half(half, own, 0, weight_ref, frames, folded)
        swap(half).wait_recv()
        filter_half(half, other, 4, weight_ref, frames, folded)

    fold(0)
    for quarter in range(CHUNKS):
        load_table(quarter).wait()

    @pl.loop(0, STEPS + 3)
    def _(turn):
        @pl.when(turn == CHUNKS)
        def _():
            fold(1)

        @pl.when(turn < STEPS)
        def _():
            def write(target, value):
                made[turn, target] = value

            transform_chunk(turn // CHUNKS, lax.rem(turn, CHUNKS), core, table, folded, turned, write)
            local(turn).start()
            for step in range(1, 4):
                first(turn, step, 0).start()
            for step in range(4):
                first(turn, step, 1).start()

        @pl.when((turn >= 1) & (turn <= STEPS))
        def _():
            t = turn - 1
            local(t).wait()
            for step in range(1, 4):
                first_arrival(t, step, 0).wait_recv()
            for way in range(2):
                ring(t, 0, way).start()
            pair(t, 0).start()
            for step in range(4):
                first_arrival(t, step, 1).wait_recv()
            pair(t, 1).start()

        @pl.when((turn >= 2) & (turn <= STEPS + 1))
        def _():
            t = turn - 2
            pair(t, 1, False).wait_recv()
            for way in range(2):
                ring(t, 1, way).start()

        @pl.when(turn >= 3)
        def _():
            t = turn - 3
            for part in range(2):
                ring(t, part, part).wait_recv()
                onward(t, part).start()

    for part in range(2):
        swap(part).wait_send()

    @pl.loop(0, STEPS)
    def _(t):
        pair(t, 0, False).wait_recv()
        for part in range(2):
            ring(t, part, 1 - part).wait_recv()
            onward(t, part).wait_recv()
        for step in range(1, 4):
            first(t, step, 0).wait_send()
        for step in range(4):
            first(t, step, 1).wait_send()
        for part in range(2):
            pair(t, part).wait_send()
            for way in range(2):
                ring(t, part, way).wait_send()
            onward(t, part).wait_send()


def exchange(voltages, weights, table):
    any_space = pl.BlockSpec(memory_space=pl.ANY)
    dma = pltpu.SemaphoreType.DMA
    return pl.pallas_call(
        exchange_kernel,
        in_specs=[any_space, pl.BlockSpec(memory_space=pltpu.VMEM), any_space],
        out_specs=[any_space, any_space],
        out_shape=[
            jax.ShapeDtypeStruct((CHUNKS, 2 * CHUNK_CHAN, 2, 4, 2, 8, SPEC), BF16),
            jax.ShapeDtypeStruct((3, CHUNKS, 2 * CHUNK_CHAN, 4, 2, 8, SPEC), BF16),
        ],
        scratch_shapes=[
            pltpu.VMEM(voltages.shape, BF16),
            pltpu.VMEM(voltages.shape, BF16),
            pltpu.VMEM(table.shape[1:], BF16),
            pltpu.VMEM((2, 4 * 132, 128), F32),
            pltpu.VMEM((2, 2, 2, 4, 2 * HALF_SPEC, HALF), BF16),
            pltpu.VMEM((TARGETS * CHUNK_CHAN * 16, 128), F32),
            pltpu.VMEM((STEPS, TARGETS, 2 * CHUNK_CHAN, 8, HALF_SPEC), BF16),
            dma((2,)),
            dma((CHUNKS,)),
            dma((2,)),
            dma((2,)),
            dma((STEPS,)),
            dma((STEPS, 8)),
            dma((STEPS, 8)),
            dma((STEPS, 2)),
            dma((STEPS, 2)),
            dma((STEPS, 2, 2)),
            dma((STEPS, 2, 2)),
            dma((STEPS, 2)),
            dma((STEPS, 2)),
        ],
        compiler_params=pltpu.CompilerParams(collective_id=0, has_side_effects=True, vmem_limit_bytes=56 << 20),
        name="exchange",
    )(voltages, weights, table)


def correlate_kernel(place_ref, rows_hbm, planes_hbm, out_hbm, rows_ref, planes_ref, out_ref, rows_sem, planes_sem, out_sem):
    z, xl = place_ref[0], place_ref[1]

    def channels(g):
        return pl.ds(g * STEP_CHAN, STEP_CHAN)

    def load_rows(g):
        return pltpu.make_async_copy(rows_hbm.at[channels(g)], rows_ref.at[channels(g)], rows_sem.at[g])

    def load_planes(g):
        return pltpu.make_async_copy(planes_hbm.at[:, channels(g)], planes_ref.at[:, channels(g)], planes_sem.at[g])

    def store(g):
        return pltpu.make_async_copy(out_ref.at[channels(g)], out_hbm.at[channels(g)], out_sem.at[g])

    groups = LOCAL_CHAN // STEP_CHAN

    @pl.loop(0, groups)
    def _(g):
        load_rows(g).start()
        load_planes(g).start()

    @pl.loop(0, groups)
    def _(g):
        load_rows(g).wait()
        load_planes(g).wait()
        for index in range(STEP_CHAN):
            c = g * STEP_CHAN + index
            real, imag = rows_ref[c, 0], rows_ref[c, 1]
            weights = jnp.concatenate(
                [jnp.concatenate([real, imag], axis=1), jnp.concatenate([imag, -real], axis=1)], axis=0
            )
            start = pl.multiple_of(xl * 64, 64)
            parts = []
            for part in range(2):
                pieces = [rows_ref[c, part, pl.ds(start, 64)]]
                pieces += [planes_ref[slot, c, part] for slot in range(3)]
                parts.append(jnp.concatenate(pieces, axis=0))
            value = lax.dot_general(
                jnp.concatenate(parts, axis=1), weights, (((1,), (1,)), ((), ())), preferred_element_type=F32
            )
            value = value * (1.0 / SPEC)
            for index, shift in enumerate((0, 3, 1, 2)):
                plane = lax.rem(z + shift, 4)
                out_ref[c, 0, plane] = value[index * 64 : index * 64 + 64, :128]
                out_ref[c, 1, plane] = value[index * 64 : index * 64 + 64, 128:]
        store(g).start()

    @pl.loop(0, groups)
    def _(g):
        store(g).wait()


def correlate(rows, planes, place):
    any_space = pl.BlockSpec(memory_space=pl.ANY)
    groups = LOCAL_CHAN // STEP_CHAN
    return pl.pallas_call(
        correlate_kernel,
        in_specs=[pl.BlockSpec(memory_space=pltpu.SMEM), any_space, any_space],
        out_specs=any_space,
        out_shape=jax.ShapeDtypeStruct((LOCAL_CHAN, 2, 4, 64, 128), F32),
        scratch_shapes=[
            pltpu.VMEM(rows.shape, BF16),
            pltpu.VMEM(planes.shape, BF16),
            pltpu.VMEM((LOCAL_CHAN, 2, 4, 64, 128), F32),
            pltpu.SemaphoreType.DMA((groups,)),
            pltpu.SemaphoreType.DMA((groups,)),
            pltpu.SemaphoreType.DMA((groups,)),
        ],
        compiler_params=pltpu.CompilerParams(vmem_limit_bytes=58 << 20),
        name="correlate",
    )(place, rows, planes)


def shards(table, voltages, tap_table):
    z, xl = lax.axis_index("row"), lax.axis_index("col")
    weights = tap_table.astype(F32)
    rows, planes = exchange(jnp.transpose(voltages, (1, 0, 2)), weights, table)
    rows = rows.reshape(LOCAL_CHAN, 2, 128, SPEC)
    planes = planes.reshape(3, LOCAL_CHAN, 2, 64, SPEC)
    return correlate(rows, planes, jnp.stack([z, xl]).astype(jnp.int32))


def solution(mesh):
    table = dft_tables()

    def run(voltages, tap_table):
        return jax.shard_map(
            shards,
            mesh=mesh,
            in_specs=(P(), P(("row", "col", "freq"), None, None), P()),
            out_specs=P("freq", None, None, "col", "row"),
            check_vma=False,
        )(jnp.asarray(table), voltages, tap_table)

    return run
```

time: 916 us -> 187 us (0.20)
  waiting for transfers between devices: 639 us -> 0 us
  Pallas kernels: 0 us -> 184 us
  matrix products: 106 us -> 0 us
  blocking collectives: 57.6 us -> 0 us
  other arithmetic: 56.4 us -> 1.97 us
  local copies, waits for them, and re-layouts: 34 us -> 0 us
  between operations: 13.9 us -> 0.01 us
    all_gather x1 -> x0, waiting for transfers between devices: 639 us -> none  [shards(): everyone = lax.all_gather(turned_block, ('row', 'col'), axis=2, tiled=True)]
    pallas_call x0 -> x2, Pallas kernels: none -> 184 us  [the longest x1 170 us: exchange(): pl.pallas_call(exchange_kernel, in_specs=[any_space, pl.BlockSpec(memory_...]
    dot_general x2 -> x0, matrix products: 106 us -> none  [the longest x1 84.8 us: shards(): jnp.einsum('cpn,isn->cpis', table, filtered, precision=lax.Precision.HIGH...]
    all_to_all x1 -> x0, blocking collectives: 57.6 us -> none  [shards(): lax.all_to_all(spectra, 'freq', split_axis=0, concat_axis=2, tiled=True)]
    mul x1 -> x0, other arithmetic: 33.1 us -> none  [dft_table(): -jnp.sin(angle) * factor]
    all_to_all x2 -> x0, local copies, waits for them, and re-layouts: 11.3 us -> none  [shards(): lax.all_to_all(spectra, 'freq', split_axis=0, concat_axis=2, tiled=True)]
    add x1 -> x0, other arithmetic: 10.2 us -> none  [shards(): filtered + weights[tap_index] * voltages[:, tap_index:tap_index + spec_co...]
  transfers between devices with their start and end apart: 1 -> 0, of which waited for: 1 -> 0; matrix products, arithmetic and copies ran while one was open for 0% -> 0% of each run, Pallas kernels for 0% -> 0%
where the time goes in v2:
time: 187 us; the launch traced here: 186 us
  Pallas kernels  184 us (98%)
  other arithmetic  1.97 us (1%)
    pallas_call x1, Pallas kernels, exchange(): pl.pallas_call(exchange_kernel, in_specs=[any_space, pl.BlockSpec(memory_...  170 us
    pallas_call x1, Pallas kernels, correlate(): pl.pallas_call(correlate_kernel, in_specs=[pl.BlockSpec(memory_space=pltp...  14.5 us

profile of v2, /device:TPU:2, one launch (start us, length us, event | category | flops | bytes accessed | tf_op | source)
XLA Modules:
  0.0 186.4 jit_solution(7833225391334173141)
XLA Ops:
  0.0 0.6 pad_add_fusion.place_ref
  0.6 1.4 convert_element_type.3.weight_ref
  2.0 169.9 %exchange.1 = (bf16[4,32,2,4,2,8,256]{6,5,4,3,2,1,0:T(8,128)(2,1)}, bf16[3,4,32,4,2,8,256]{6,5,4,3,2,1,0:T(8,128)(2,1)}) custom-call(bf16[259,4,2048]{2,1,0:T(4,128)(2,1)} %bitcast.7, f32[4,2048]{1,0:T(4,128)} %convert_element_type.3.weight_ref, bf16[2,4,2,256,1024]{4,3,2,1,0:T(8,128)(2,1)} %constant.10.clone.table_hbm), custom_call_target="tpu_custom_call" | custom-call | tf_op jit(solution)/shard_map/exchange/pallas_call | solution.py:284
  171.9 14.5 %correlate.1 = f32[64,2,4,64,128]{4,3,2,1,0:T(8,128)} custom-call(s32[2]{0:T(128)} %pad_add_fusion.place_ref, bf16[64,2,128,256]{3,2,1,0:T(8,128)(2,1)} %bitcast.6, bf16[3,64,2,64,256]{4,3,2,1,0:T(8,128)(2,1)} %bitcast.5), custom_call_target="tpu_custom_call" | custom-call | tf_op jit(solution)/shard_map/correlate/pallas_call | solution.py:375

commit v3 on v2

--- a/solution.py
+++ b/solution.py
@@ -102,11 +102,16 @@
         write(target, rows.reshape(2 * CHUNK_CHAN, 8, 128).astype(BF16))
 
 
+def stacked(real, imag):
+    return jnp.concatenate([jnp.concatenate([real, imag], axis=1), jnp.concatenate([imag, -real], axis=1)], axis=0)
+
+
 def exchange_kernel(
-    own_ref, weight_ref, table_hbm, rows, planes,
-    own, other, table, frames, folded, turned, made,
+    own_ref, weight_ref, table_hbm, rows, near, far, crossed,
+    own, other, table, frames, folded, turned, made, rows_part, near_part, products,
     load_sem, table_sem, core_send, core_recv,
     local_sem, first_send, first_recv, pair_send, pair_recv, ring_send, ring_recv, pass_send, pass_recv,
+    part_sem, back_send, back_recv,
 ):
     freq, z, xl = lax.axis_index("freq"), lax.axis_index("row"), lax.axis_index("col")
     core = lax.rem(freq, 2)
@@ -137,7 +142,7 @@
     others = [sibling]
     others += [device(lax.rem(y + step, 4), xh, z, xl) for step in range(1, 4)]
     others += [device(lax.rem(y + step, 4), 1 - xh, z, 1 - xl) for step in range(4)]
-    others += [partner, above, below]
+    others += [partner, above, below, device(y, xh, up, 1 - xl), device(y, xh, down, 1 - xl)]
     for one in others:
         pl.semaphore_signal(barrier, inc=1, device_id=one, device_id_type=MESH)
     pl.semaphore_wait(barrier, len(others))
@@ -156,7 +161,7 @@
         swap(part).start()
 
     def spot(t):
-        return lax.rem(t, CHUNKS), pl.ds(pl.multiple_of((t // CHUNKS) * HALF_SPEC, HALF_SPEC), HALF_SPEC)
+        return t // 2, pl.ds(pl.multiple_of(lax.rem(t, 2) * HALF_SPEC, HALF_SPEC), HALF_SPEC)
 
     def home(t, side, from_y, from_xh):
         k, lanes = spot(t)
@@ -190,18 +195,62 @@
     def ring(t, part, way):
         k, lanes = spot(t)
         column = xh if part == 0 else 1 - xh
-        return remote(
-            rows.at[k, :, xl, :, column, :, lanes], planes.at[way, k, :, :, column, :, lanes],
+        share = pl.ds(way * CHUNK_CHAN, CHUNK_CHAN)
+        return remote(
+            rows.at[k, share, xl, :, column, :, lanes], near.at[k, share, :, column, :, lanes],
             ring_send.at[t, part, way], ring_recv.at[t, part, way], above if way == 0 else below,
         )
 
-    def onward(t, part):
+    def onward(t, part, way):
         k, lanes = spot(t)
         column = xh if part == 0 else 1 - xh
-        return remote(
-            planes.at[part, k, :, :, column, :, lanes], planes.at[2, k, :, :, column, :, lanes],
-            pass_send.at[t, part], pass_recv.at[t, part], above if part == 0 else below,
-        )
+        share = pl.ds(way * CHUNK_CHAN, CHUNK_CHAN)
+        return remote(
+            near.at[k, share, :, column, :, lanes], far.at[k, share, :, column, :, lanes],
+            pass_send.at[t, part, way], pass_recv.at[t, part, way], above if way == 0 else below,
+        )
+
+    def back(k, way, side):
+        share = pl.ds(way * FOLD_CHAN, FOLD_CHAN)
+        return remote(
+            products.at[k, side, share], crossed.at[xl, k, share],
+            back_send.at[k, way, side], back_recv.at[k, way, xl],
+            device(y, xh, down if way == 0 else up, side),
+        )
+
+    def back_arrival(k, way, side):
+        share = pl.ds(way * FOLD_CHAN, FOLD_CHAN)
+        place = crossed.at[side, k, share]
+        return remote(
+            place, place, back_send.at[k, way, side], back_recv.at[k, way, side],
+            device(y, xh, up if way == 0 else down, side),
+        )
+
+    def multiply(k):
+        copies = [
+            pltpu.make_async_copy(rows.at[k], rows_part, part_sem.at[0]),
+            pltpu.make_async_copy(near.at[k], near_part, part_sem.at[1]),
+        ]
+        for copy in copies:
+            copy.start()
+        for copy in copies:
+            copy.wait()
+
+        @pl.loop(0, CHUNK_CHAN)
+        def _(c):
+            left = [rows_part[2 * c + part].reshape(128, SPEC) for part in range(2)]
+            right = [near_part[2 * c + part].reshape(64, SPEC) for part in range(2)]
+            value = lax.dot_general(
+                jnp.concatenate(left, axis=1), stacked(right[0], right[1]), (((1,), (1,)), ((), ())),
+                preferred_element_type=F32,
+            )
+            value = (value * (1.0 / SPEC)).astype(BF16)
+            products[k, 0, c] = value[:64]
+            products[k, 1, c] = value[64:]
+
+        for way in range(2):
+            for side in range(2):
+                back(k, way, side).start()
 
     def fold(half):
         load(half).wait()
@@ -213,9 +262,9 @@
     for quarter in range(CHUNKS):
         load_table(quarter).wait()
 
-    @pl.loop(0, STEPS + 3)
+    @pl.loop(0, STEPS + 4)
     def _(turn):
-        @pl.when(turn == CHUNKS)
+        @pl.when(turn == 1)
         def _():
             fold(1)
 
@@ -224,7 +273,7 @@
             def write(target, value):
                 made[turn, target] = value
 
-            transform_chunk(turn // CHUNKS, lax.rem(turn, CHUNKS), core, table, folded, turned, write)
+            transform_chunk(lax.rem(turn, 2), turn // 2, core, table, folded, turned, write)
             local(turn).start()
             for step in range(1, 4):
                 first(turn, step, 0).start()
@@ -251,22 +300,31 @@
             for way in range(2):
                 ring(t, 1, way).start()
 
-        @pl.when(turn >= 3)
+        @pl.when((turn >= 3) & (turn <= STEPS + 2))
         def _():
             t = turn - 3
             for part in range(2):
-                ring(t, part, part).wait_recv()
-                onward(t, part).start()
+                for way in range(2):
+                    ring(t, part, way).wait_recv()
+                    onward(t, part, way).start()
+            pair(t, 0, False).wait_recv()
+
+        @pl.when((turn >= 5) & (lax.rem(turn, 2) == 1))
+        def _():
+            multiply((turn - 5) // 2)
 
     for part in range(2):
         swap(part).wait_send()
 
+    @pl.loop(0, CHUNKS)
+    def _(k):
+        for way in range(2):
+            for side in range(2):
+                back_arrival(k, way, side).wait_recv()
+                back(k, way, side).wait_send()
+
     @pl.loop(0, STEPS)
     def _(t):
-        pair(t, 0, False).wait_recv()
-        for part in range(2):
-            ring(t, part, 1 - part).wait_recv()
-            onward(t, part).wait_recv()
         for step in range(1, 4):
             first(t, step, 0).wait_send()
         for step in range(4):
@@ -275,7 +333,8 @@
             pair(t, part).wait_send()
             for way in range(2):
                 ring(t, part, way).wait_send()
-            onward(t, part).wait_send()
+                onward(t, part, way).wait_recv()
+                onward(t, part, way).wait_send()
 
 
 def exchange(voltages, weights, table):
@@ -284,10 +343,12 @@
     return pl.pallas_call(
         exchange_kernel,
         in_specs=[any_space, pl.BlockSpec(memory_space=pltpu.VMEM), any_space],
-        out_specs=[any_space, any_space],
+        out_specs=[any_space] * 4,
         out_shape=[
             jax.ShapeDtypeStruct((CHUNKS, 2 * CHUNK_CHAN, 2, 4, 2, 8, SPEC), BF16),
-            jax.ShapeDtypeStruct((3, CHUNKS, 2 * CHUNK_CHAN, 4, 2, 8, SPEC), BF16),
+            jax.ShapeDtypeStruct((CHUNKS, 2 * CHUNK_CHAN, 4, 2, 8, SPEC), BF16),
+            jax.ShapeDtypeStruct((CHUNKS, 2 * CHUNK_CHAN, 4, 2, 8, SPEC), BF16),
+            jax.ShapeDtypeStruct((2, CHUNKS, CHUNK_CHAN, 64, 128), BF16),
         ],
         scratch_shapes=[
             pltpu.VMEM(voltages.shape, BF16),
@@ -297,6 +358,9 @@
             pltpu.VMEM((2, 2, 2, 4, 2 * HALF_SPEC, HALF), BF16),
             pltpu.VMEM((TARGETS * CHUNK_CHAN * 16, 128), F32),
             pltpu.VMEM((STEPS, TARGETS, 2 * CHUNK_CHAN, 8, HALF_SPEC), BF16),
+            pltpu.VMEM((2 * CHUNK_CHAN, 2, 4, 2, 8, SPEC), BF16),
+            pltpu.VMEM((2 * CHUNK_CHAN, 4, 2, 8, SPEC), BF16),
+            pltpu.VMEM((CHUNKS, 2, CHUNK_CHAN, 64, 128), BF16),
             dma((2,)),
             dma((CHUNKS,)),
             dma((2,)),
@@ -308,25 +372,31 @@
             dma((STEPS, 2)),
             dma((STEPS, 2, 2)),
             dma((STEPS, 2, 2)),
-            dma((STEPS, 2)),
-            dma((STEPS, 2)),
+            dma((STEPS, 2, 2)),
+            dma((STEPS, 2, 2)),
+            dma((2,)),
+            dma((CHUNKS, 2, 2)),
+            dma((CHUNKS, 2, 2)),
         ],
         compiler_params=pltpu.CompilerParams(collective_id=0, has_side_effects=True, vmem_limit_bytes=56 << 20),
         name="exchange",
     )(voltages, weights, table)
 
 
-def correlate_kernel(place_ref, rows_hbm, planes_hbm, out_hbm, rows_ref, planes_ref, out_ref, rows_sem, planes_sem, out_sem):
+def correlate_kernel(
+    place_ref, rows_hbm, near_hbm, far_hbm, crossed_hbm, out_hbm,
+    rows_ref, near_ref, far_ref, crossed_ref, out_ref, load_sem, out_sem,
+):
     z, xl = place_ref[0], place_ref[1]
 
     def channels(g):
         return pl.ds(g * STEP_CHAN, STEP_CHAN)
 
-    def load_rows(g):
-        return pltpu.make_async_copy(rows_hbm.at[channels(g)], rows_ref.at[channels(g)], rows_sem.at[g])
-
-    def load_planes(g):
-        return pltpu.make_async_copy(planes_hbm.at[:, channels(g)], planes_ref.at[:, channels(g)], planes_sem.at[g])
+    def loads(g):
+        some = channels(g)
+        pairs = [(rows_hbm.at[some], rows_ref.at[some]), (near_hbm.at[some], near_ref.at[some])]
+        pairs += [(far_hbm.at[some], far_ref.at[some]), (crossed_hbm.at[:, some], crossed_ref.at[:, some])]
+        return [pltpu.make_async_copy(a, b, load_sem.at[g, i]) for i, (a, b) in enumerate(pairs)]
 
     def store(g):
         return pltpu.make_async_copy(out_ref.at[channels(g)], out_hbm.at[channels(g)], out_sem.at[g])
@@ -335,33 +405,35 @@
 
     @pl.loop(0, groups)
     def _(g):
-        load_rows(g).start()
-        load_planes(g).start()
+        for copy in loads(g):
+            copy.start()
 
     @pl.loop(0, groups)
     def _(g):
-        load_rows(g).wait()
-        load_planes(g).wait()
+        for copy in loads(g):
+            copy.wait()
+        down_share = lax.rem(g // (FOLD_CHAN // STEP_CHAN), 2)
+        near_plane = lax.rem(z + 3 + 2 * down_share, 4)
+        far_plane = lax.rem(z + 2, 4)
+        crossed_plane = lax.rem(z + 1 + 2 * down_share, 4)
         for index in range(STEP_CHAN):
             c = g * STEP_CHAN + index
-            real, imag = rows_ref[c, 0], rows_ref[c, 1]
-            weights = jnp.concatenate(
-                [jnp.concatenate([real, imag], axis=1), jnp.concatenate([imag, -real], axis=1)], axis=0
-            )
             start = pl.multiple_of(xl * 64, 64)
             parts = []
             for part in range(2):
-                pieces = [rows_ref[c, part, pl.ds(start, 64)]]
-                pieces += [planes_ref[slot, c, part] for slot in range(3)]
+                pieces = [rows_ref[c, part, pl.ds(start, 64)], near_ref[c, part], far_ref[c, part]]
                 parts.append(jnp.concatenate(pieces, axis=0))
             value = lax.dot_general(
-                jnp.concatenate(parts, axis=1), weights, (((1,), (1,)), ((), ())), preferred_element_type=F32
+                jnp.concatenate(parts, axis=1), stacked(rows_ref[c, 0], rows_ref[c, 1]), (((1,), (1,)), ((), ())),
+                preferred_element_type=F32,
             )
             value = value * (1.0 / SPEC)
-            for index, shift in enumerate((0, 3, 1, 2)):
-                plane = lax.rem(z + shift, 4)
+            for index, plane in enumerate((z, near_plane, far_plane)):
                 out_ref[c, 0, plane] = value[index * 64 : index * 64 + 64, :128]
                 out_ref[c, 1, plane] = value[index * 64 : index * 64 + 64, 128:]
+            sides = [crossed_ref[side, c].astype(F32) for side in range(2)]
+            out_ref[c, 0, crossed_plane] = jnp.concatenate([side[:, :64] for side in sides], axis=1)
+            out_ref[c, 1, crossed_plane] = jnp.concatenate([side[:, 64:] for side in sides], axis=1)
         store(g).start()
 
     @pl.loop(0, groups)
@@ -369,34 +441,37 @@
         store(g).wait()
 
 
-def correlate(rows, planes, place):
+def correlate(rows, near, far, crossed, place):
     any_space = pl.BlockSpec(memory_space=pl.ANY)
     groups = LOCAL_CHAN // STEP_CHAN
     return pl.pallas_call(
         correlate_kernel,
-        in_specs=[pl.BlockSpec(memory_space=pltpu.SMEM), any_space, any_space],
+        in_specs=[pl.BlockSpec(memory_space=pltpu.SMEM)] + [any_space] * 4,
         out_specs=any_space,
         out_shape=jax.ShapeDtypeStruct((LOCAL_CHAN, 2, 4, 64, 128), F32),
         scratch_shapes=[
             pltpu.VMEM(rows.shape, BF16),
-            pltpu.VMEM(planes.shape, BF16),
+            pltpu.VMEM(near.shape, BF16),
+            pltpu.VMEM(far.shape, BF16),
+            pltpu.VMEM(crossed.shape, BF16),
             pltpu.VMEM((LOCAL_CHAN, 2, 4, 64, 128), F32),
-            pltpu.SemaphoreType.DMA((groups,)),
-            pltpu.SemaphoreType.DMA((groups,)),
+            pltpu.SemaphoreType.DMA((groups, 4)),
             pltpu.SemaphoreType.DMA((groups,)),
         ],
         compiler_params=pltpu.CompilerParams(vmem_limit_bytes=58 << 20),
         name="correlate",
-    )(place, rows, planes)
+    )(place, rows, near, far, crossed)
 
 
 def shards(table, voltages, tap_table):
     z, xl = lax.axis_index("row"), lax.axis_index("col")
     weights = tap_table.astype(F32)
-    rows, planes = exchange(jnp.transpose(voltages, (1, 0, 2)), weights, table)
+    rows, near, far, crossed = exchange(jnp.transpose(voltages, (1, 0, 2)), weights, table)
     rows = rows.reshape(LOCAL_CHAN, 2, 128, SPEC)
-    planes = planes.reshape(3, LOCAL_CHAN, 2, 64, SPEC)
-    return correlate(rows, planes, jnp.stack([z, xl]).astype(jnp.int32))
+    near = near.reshape(LOCAL_CHAN, 2, 64, SPEC)
+    far = far.reshape(LOCAL_CHAN, 2, 64, SPEC)
+    crossed = crossed.reshape(2, LOCAL_CHAN, 64, 128)
+    return correlate(rows, near, far, crossed, jnp.stack([z, xl]).astype(jnp.int32))
 
 
 def solution(mesh):

time: 187 us -> 184 us (0.984)
  Pallas kernels: 184 us -> 182 us
    pallas_call x1, Pallas kernels: 170 us -> 168 us  [exchange(): pl.pallas_call(exchange_kernel, in_specs=[any_space, pl.BlockSpec(memory_...]
where the time goes in v3:
time: 184 us
  Pallas kernels  182 us (99%)
  other arithmetic  1.97 us (1%)
    pallas_call x1, Pallas kernels, exchange(): pl.pallas_call(exchange_kernel, in_specs=[any_space, pl.BlockSpec(memory_...  168 us
    pallas_call x1, Pallas kernels, correlate(): pl.pallas_call(correlate_kernel, in_specs=[pl.BlockSpec(memory_space=pltp...  14 us

profile of v3, /device:TPU:2, one launch (start us, length us, event | category | flops | bytes accessed | tf_op | source)
XLA Modules:
  0.0 183.8 jit_solution(6342073360531477315)
XLA Ops:
  0.0 0.6 pad_add_fusion.place_ref
  0.6 1.4 convert_element_type.3.weight_ref
  2.0 167.9 %exchange.1 = (bf16[4,32,2,4,2,8,256]{6,5,4,3,2,1,0:T(8,128)(2,1)}, bf16[4,32,4,2,8,256]{5,4,3,2,1,0:T(8,128)(2,1)}, bf16[4,32,4,2,8,256]{5,4,3,2,1,0:T(8,128)(2,1)}, bf16[2,4,16,64,128]{4,3,2,1,0:T(8,128)(2,1)}) custom-call(bf16[259,4,2048]{2,1,0:T(4,128)(2,1)} %bitcast.8, f32[4,2048]{1,0:T(4,128)} %convert_element_type.3.weight_ref, ...), custom_call_target="tpu_custom_call" | custom-call | tf_op jit(solution)/shard_map/exchange/pallas_call | solution.py:343
  169.8 14.0 %correlate.1 = f32[64,2,4,64,128]{4,3,2,1,0:T(8,128)} custom-call(s32[2]{0:T(128)} %pad_add_fusion.place_ref, bf16[64,2,128,256]{3,2,1,0:T(8,128)(2,1)} %bitcast.7, bf16[64,2,64,256]{3,2,1,0:T(8,128)(2,1)} %bitcast.9, bf16[64,2,64,256]{3,2,1,0:T(8,128)(2,1)} %bitcast.10, bf16[2,64,64,128]{3,2,1,0:T(8,128)(2,1)} %bitcast.11), custom_call_target="tpu_custom_call" | custom-call | tf_op jit(solution)/shard_map/correlate/pallas_call | solution.py:447

commit v4 on v3

--- a/solution.py
+++ b/solution.py
@@ -24,6 +24,9 @@
 HALF_SPEC = SPEC // 2
 STEPS = 2 * CHUNKS
 STEP_CHAN = 4
+PAIR_LAG = 2
+PASS_LAG = 3
+BACK_LAG = 4
 F32 = jnp.float32
 BF16 = jnp.bfloat16
 MESH = pl.DeviceIdType.MESH
@@ -46,33 +49,36 @@
     return np.concatenate([high.reshape(shape), low.reshape(shape)], axis=3)
 
 
-def filter_half(half, source, first, weight_ref, frames, folded):
-    count = HALF_SPEC + TAPS - 1
+def filter_half(half, source, first, taps_ref, frames, mixed, folded):
+    count = 4 * (HALF_SPEC + TAPS - 1)
 
     @pl.loop(0, HALF // 128)
     def _(step):
         low = pl.multiple_of(step * 128, 128)
         columns = (low, pl.multiple_of(low + HALF, 128))
+        weights = []
         for side in range(2):
-            block = source[pl.ds(half * HALF_SPEC, count), :, pl.ds(columns[side], 128)]
-            frames[side, 0 : 4 * count, :] = block.astype(F32).reshape(4 * count, 128)
+            block = source[pl.ds(half * HALF_SPEC, HALF_SPEC + TAPS - 1), :, pl.ds(columns[side], 128)]
+            frames[side, 0:count, :] = block.astype(F32).reshape(count, 128)
+            weights.append([taps_ref[pl.ds(tap, 1), pl.ds(columns[side], 128)].astype(F32) for tap in range(TAPS)])
+        for start in range(0, 4 * HALF_SPEC, 64):
+            sides = []
+            for side in range(2):
+                even = frames[side, start : start + 72, :]
+                odd = frames[side, start + 4 : start + 76, :]
+                w = weights[side]
+                sides.append(w[0] * even[:64] + w[1] * odd[:64] + w[2] * even[8:] + w[3] * odd[8:])
+            mixed[0, start : start + 64, :] = sides[0] + sides[1]
+            mixed[1, start : start + 64, :] = sides[0] - sides[1]
         for row in range(4):
             slot = first + row
-            for start in range(0, HALF_SPEC, 64):
-                sides = []
-                for side in range(2):
-                    total = None
-                    for tap in range(TAPS):
-                        weight = weight_ref[pl.ds(tap, 1), pl.ds(columns[side], 128)]
-                        term = weight * frames[side, pl.ds((start + tap) * 4 + row, 64, stride=4), :]
-                        total = term if total is None else total + term
-                    sides.append(total)
-                place = (slot % 2) * HALF_SPEC + start
-                for parity, value in ((0, sides[0] + sides[1]), (1, sides[0] - sides[1])):
-                    top = value.astype(BF16)
-                    rest = (value - top.astype(F32)).astype(BF16)
-                    folded[parity, 0, half, slot // 2, place : place + 64, pl.ds(low, 128)] = top
-                    folded[parity, 1, half, slot // 2, place : place + 64, pl.ds(low, 128)] = rest
+            place = (slot % 2) * HALF_SPEC
+            for parity in range(2):
+                value = mixed[parity, pl.ds(row, HALF_SPEC, stride=4), :]
+                top = value.astype(BF16)
+                rest = (value - top.astype(F32)).astype(BF16)
+                folded[parity, 0, half, slot // 2, place : place + HALF_SPEC, pl.ds(low, 128)] = top
+                folded[parity, 1, half, slot // 2, place : place + HALF_SPEC, pl.ds(low, 128)] = rest
 
 
 def transform_chunk(half, quarter, core, table_ref, folded, turned, write):
@@ -107,8 +113,8 @@
 
 
 def exchange_kernel(
-    own_ref, weight_ref, table_hbm, rows, near, far, crossed,
-    own, other, table, frames, folded, turned, made, rows_part, near_part, products,
+    own_ref, taps_ref, table_hbm, rows, near, far, crossed,
+    own, other, table, frames, mixed, folded, turned, made, rows_part, near_part, products,
     load_sem, table_sem, core_send, core_recv,
     local_sem, first_send, first_recv, pair_send, pair_recv, ring_send, ring_recv, pass_send, pass_recv,
     part_sem, back_send, back_recv,
@@ -161,7 +167,7 @@
         swap(part).start()
 
     def spot(t):
-        return t // 2, pl.ds(pl.multiple_of(lax.rem(t, 2) * HALF_SPEC, HALF_SPEC), HALF_SPEC)
+        return lax.rem(t, CHUNKS), pl.ds(pl.multiple_of((t // CHUNKS) * HALF_SPEC, HALF_SPEC), HALF_SPEC)
 
     def home(t, side, from_y, from_xh):
         k, lanes = spot(t)
@@ -254,17 +260,17 @@
 
     def fold(half):
         load(half).wait()
-        filter_half(half, own, 0, weight_ref, frames, folded)
+        filter_half(half, own, 0, taps_ref, frames, mixed, folded)
         swap(half).wait_recv()
-        filter_half(half, other, 4, weight_ref, frames, folded)
+        filter_half(half, other, 4, taps_ref, frames, mixed, folded)
 
     fold(0)
     for quarter in range(CHUNKS):
         load_table(quarter).wait()
 
-    @pl.loop(0, STEPS + 4)
+    @pl.loop(0, STEPS + BACK_LAG)
     def _(turn):
-        @pl.when(turn == 1)
+        @pl.when(turn == CHUNKS)
         def _():
             fold(1)
 
@@ -273,7 +279,7 @@
             def write(target, value):
                 made[turn, target] = value
 
-            transform_chunk(lax.rem(turn, 2), turn // 2, core, table, folded, turned, write)
+            transform_chunk(turn // CHUNKS, lax.rem(turn, CHUNKS), core, table, folded, turned, write)
             local(turn).start()
             for step in range(1, 4):
                 first(turn, step, 0).start()
@@ -288,30 +294,30 @@
                 first_arrival(t, step, 0).wait_recv()
             for way in range(2):
                 ring(t, 0, way).start()
-            pair(t, 0).start()
             for step in range(4):
                 first_arrival(t, step, 1).wait_recv()
             pair(t, 1).start()
-
-        @pl.when((turn >= 2) & (turn <= STEPS + 1))
-        def _():
-            t = turn - 2
+            pair(t, 0).start()
+
+        @pl.when((turn >= PAIR_LAG) & (turn < STEPS + PAIR_LAG))
+        def _():
+            t = turn - PAIR_LAG
             pair(t, 1, False).wait_recv()
             for way in range(2):
                 ring(t, 1, way).start()
 
-        @pl.when((turn >= 3) & (turn <= STEPS + 2))
-        def _():
-            t = turn - 3
+        @pl.when((turn >= PASS_LAG) & (turn < STEPS + PASS_LAG))
+        def _():
+            t = turn - PASS_LAG
             for part in range(2):
                 for way in range(2):
                     ring(t, part, way).wait_recv()
                     onward(t, part, way).start()
             pair(t, 0, False).wait_recv()
 
-        @pl.when((turn >= 5) & (lax.rem(turn, 2) == 1))
-        def _():
-            multiply((turn - 5) // 2)
+        @pl.when(turn >= CHUNKS + BACK_LAG)
+        def _():
+            multiply(turn - CHUNKS - BACK_LAG)
 
     for part in range(2):
         swap(part).wait_send()
@@ -337,7 +343,7 @@
                 onward(t, part, way).wait_send()
 
 
-def exchange(voltages, weights, table):
+def exchange(voltages, taps, table):
     any_space = pl.BlockSpec(memory_space=pl.ANY)
     dma = pltpu.SemaphoreType.DMA
     return pl.pallas_call(
@@ -355,6 +361,7 @@
             pltpu.VMEM(voltages.shape, BF16),
             pltpu.VMEM(table.shape[1:], BF16),
             pltpu.VMEM((2, 4 * 132, 128), F32),
+            pltpu.VMEM((2, 4 * HALF_SPEC, 128), F32),
             pltpu.VMEM((2, 2, 2, 4, 2 * HALF_SPEC, HALF), BF16),
             pltpu.VMEM((TARGETS * CHUNK_CHAN * 16, 128), F32),
             pltpu.VMEM((STEPS, TARGETS, 2 * CHUNK_CHAN, 8, HALF_SPEC), BF16),
@@ -380,14 +387,14 @@
         ],
         compiler_params=pltpu.CompilerParams(collective_id=0, has_side_effects=True, vmem_limit_bytes=56 << 20),
         name="exchange",
-    )(voltages, weights, table)
+    )(voltages, taps, table)
 
 
 def correlate_kernel(
-    place_ref, rows_hbm, near_hbm, far_hbm, crossed_hbm, out_hbm,
+    rows_hbm, near_hbm, far_hbm, crossed_hbm, out_hbm,
     rows_ref, near_ref, far_ref, crossed_ref, out_ref, load_sem, out_sem,
 ):
-    z, xl = place_ref[0], place_ref[1]
+    z, xl = lax.axis_index("row"), lax.axis_index("col")
 
     def channels(g):
         return pl.ds(g * STEP_CHAN, STEP_CHAN)
@@ -441,12 +448,12 @@
         store(g).wait()
 
 
-def correlate(rows, near, far, crossed, place):
+def correlate(rows, near, far, crossed):
     any_space = pl.BlockSpec(memory_space=pl.ANY)
     groups = LOCAL_CHAN // STEP_CHAN
     return pl.pallas_call(
         correlate_kernel,
-        in_specs=[pl.BlockSpec(memory_space=pltpu.SMEM)] + [any_space] * 4,
+        in_specs=[any_space] * 4,
         out_specs=any_space,
         out_shape=jax.ShapeDtypeStruct((LOCAL_CHAN, 2, 4, 64, 128), F32),
         scratch_shapes=[
@@ -460,18 +467,16 @@
         ],
         compiler_params=pltpu.CompilerParams(vmem_limit_bytes=58 << 20),
         name="correlate",
-    )(place, rows, near, far, crossed)
+    )(rows, near, far, crossed)
 
 
 def shards(table, voltages, tap_table):
-    z, xl = lax.axis_index("row"), lax.axis_index("col")
-    weights = tap_table.astype(F32)
-    rows, near, far, crossed = exchange(jnp.transpose(voltages, (1, 0, 2)), weights, table)
+    rows, near, far, crossed = exchange(jnp.transpose(voltages, (1, 0, 2)), tap_table, table)
     rows = rows.reshape(LOCAL_CHAN, 2, 128, SPEC)
     near = near.reshape(LOCAL_CHAN, 2, 64, SPEC)
     far = far.reshape(LOCAL_CHAN, 2, 64, SPEC)
     crossed = crossed.reshape(2, LOCAL_CHAN, 64, 128)
-    return correlate(rows, near, far, crossed, jnp.stack([z, xl]).astype(jnp.int32))
+    return correlate(rows, near, far, crossed)
 
 
 def solution(mesh):

time: 184 us -> 170 us (0.924)
  Pallas kernels: 182 us -> 170 us
  other arithmetic: 1.97 us -> 0 us
    pallas_call x1, Pallas kernels: 168 us -> 157 us  [exchange(): pl.pallas_call(exchange_kernel, in_specs=[any_space, pl.BlockSpec(memory_...]
where the time goes in v4:
time: 170 us
  Pallas kernels  170 us (100%)
    pallas_call x1, Pallas kernels, exchange(): pl.pallas_call(exchange_kernel, in_specs=[any_space, pl.BlockSpec(memory_...  157 us
    pallas_call x1, Pallas kernels, correlate(): pl.pallas_call(correlate_kernel, in_specs=[any_space] * 4, out_specs=any_...  13.3 us

profile of v4, /device:TPU:2, one launch (start us, length us, event | category | flops | bytes accessed | tf_op | source)
XLA Modules:
  0.0 170.0 jit_solution(2226336727187020156)
XLA Ops:
  0.0 156.6 %exchange.1 = (bf16[4,32,2,4,2,8,256]{6,5,4,3,2,1,0:T(8,128)(2,1)}, bf16[4,32,4,2,8,256]{5,4,3,2,1,0:T(8,128)(2,1)}, bf16[4,32,4,2,8,256]{5,4,3,2,1,0:T(8,128)(2,1)}, bf16[2,4,16,64,128]{4,3,2,1,0:T(8,128)(2,1)}) custom-call(bf16[259,4,2048]{2,1,0:T(4,128)(2,1)} %bitcast.6, s32[4,2048]{1,0:T(4,128)} %taps_ref.1, ...), custom_call_target="tpu_custom_call" | custom-call | tf_op jit(solution)/shard_map/exchange/pallas_call | solution.py:349
  156.6 13.3 %correlate.1 = f32[64,2,4,64,128]{4,3,2,1,0:T(8,128)} custom-call(bf16[64,2,128,256]{3,2,1,0:T(8,128)(2,1)} %bitcast.5, bf16[64,2,64,256]{3,2,1,0:T(8,128)(2,1)} %bitcast.7, bf16[64,2,64,256]{3,2,1,0:T(8,128)(2,1)} %bitcast.8, bf16[2,64,64,128]{3,2,1,0:T(8,128)(2,1)} %bitcast.9), custom_call_target="tpu_custom_call" | custom-call | tf_op jit(solution)/shard_map/correlate/pallas_call | solution.py:454

commit v5 on v4

--- a/solution.py
+++ b/solution.py
@@ -24,6 +24,7 @@
 HALF_SPEC = SPEC // 2
 STEPS = 2 * CHUNKS
 STEP_CHAN = 4
+SLOTS = 6
 PAIR_LAG = 2
 PASS_LAG = 3
 BACK_LAG = 4
@@ -114,10 +115,10 @@
 
 def exchange_kernel(
     own_ref, taps_ref, table_hbm, rows, near, far, crossed,
-    own, other, table, frames, mixed, folded, turned, made, rows_part, near_part, products,
+    own, other, table, frames, mixed, folded, turned, made, products,
     load_sem, table_sem, core_send, core_recv,
     local_sem, first_send, first_recv, pair_send, pair_recv, ring_send, ring_recv, pass_send, pass_recv,
-    part_sem, back_send, back_recv,
+    back_send, back_recv,
 ):
     freq, z, xl = lax.axis_index("freq"), lax.axis_index("row"), lax.axis_index("col")
     core = lax.rem(freq, 2)
@@ -233,19 +234,10 @@
         )
 
     def multiply(k):
-        copies = [
-            pltpu.make_async_copy(rows.at[k], rows_part, part_sem.at[0]),
-            pltpu.make_async_copy(near.at[k], near_part, part_sem.at[1]),
-        ]
-        for copy in copies:
-            copy.start()
-        for copy in copies:
-            copy.wait()
-
         @pl.loop(0, CHUNK_CHAN)
         def _(c):
-            left = [rows_part[2 * c + part].reshape(128, SPEC) for part in range(2)]
-            right = [near_part[2 * c + part].reshape(64, SPEC) for part in range(2)]
+            left = [rows[k, 2 * c + part].reshape(128, SPEC) for part in range(2)]
+            right = [near[k, 2 * c + part].reshape(64, SPEC) for part in range(2)]
             value = lax.dot_general(
                 jnp.concatenate(left, axis=1), stacked(right[0], right[1]), (((1,), (1,)), ((), ())),
                 preferred_element_type=F32,
@@ -349,12 +341,12 @@
     return pl.pallas_call(
         exchange_kernel,
         in_specs=[any_space, pl.BlockSpec(memory_space=pltpu.VMEM), any_space],
-        out_specs=[any_space] * 4,
+        out_specs=[pl.BlockSpec(memory_space=pltpu.VMEM)] * 4,
         out_shape=[
-            jax.ShapeDtypeStruct((CHUNKS, 2 * CHUNK_CHAN, 2, 4, 2, 8, SPEC), BF16),
-            jax.ShapeDtypeStruct((CHUNKS, 2 * CHUNK_CHAN, 4, 2, 8, SPEC), BF16),
-            jax.ShapeDtypeStruct((CHUNKS, 2 * CHUNK_CHAN, 4, 2, 8, SPEC), BF16),
-            jax.ShapeDtypeStruct((2, CHUNKS, CHUNK_CHAN, 64, 128), BF16),
+            pltpu.VMEM((CHUNKS, 2 * CHUNK_CHAN, 2, 4, 2, 8, SPEC), BF16),
+            pltpu.VMEM((CHUNKS, 2 * CHUNK_CHAN, 4, 2, 8, SPEC), BF16),
+            pltpu.VMEM((CHUNKS, 2 * CHUNK_CHAN, 4, 2, 8, SPEC), BF16),
+            pltpu.VMEM((2, CHUNKS, CHUNK_CHAN, 64, 128), BF16),
         ],
         scratch_shapes=[
             pltpu.VMEM(voltages.shape, BF16),
@@ -365,8 +357,6 @@
             pltpu.VMEM((2, 2, 2, 4, 2 * HALF_SPEC, HALF), BF16),
             pltpu.VMEM((TARGETS * CHUNK_CHAN * 16, 128), F32),
             pltpu.VMEM((STEPS, TARGETS, 2 * CHUNK_CHAN, 8, HALF_SPEC), BF16),
-            pltpu.VMEM((2 * CHUNK_CHAN, 2, 4, 2, 8, SPEC), BF16),
-            pltpu.VMEM((2 * CHUNK_CHAN, 4, 2, 8, SPEC), BF16),
             pltpu.VMEM((CHUNKS, 2, CHUNK_CHAN, 64, 128), BF16),
             dma((2,)),
             dma((CHUNKS,)),
@@ -381,101 +371,80 @@
             dma((STEPS, 2, 2)),
             dma((STEPS, 2, 2)),
             dma((STEPS, 2, 2)),
-            dma((2,)),
             dma((CHUNKS, 2, 2)),
             dma((CHUNKS, 2, 2)),
         ],
-        compiler_params=pltpu.CompilerParams(collective_id=0, has_side_effects=True, vmem_limit_bytes=56 << 20),
+        compiler_params=pltpu.CompilerParams(collective_id=0, has_side_effects=True, vmem_limit_bytes=40 << 20),
         name="exchange",
     )(voltages, taps, table)
 
 
-def correlate_kernel(
-    rows_hbm, near_hbm, far_hbm, crossed_hbm, out_hbm,
-    rows_ref, near_ref, far_ref, crossed_ref, out_ref, load_sem, out_sem,
-):
+def correlate_kernel(rows, near, far, crossed, out_hbm, out_ref, out_sem):
     z, xl = lax.axis_index("row"), lax.axis_index("col")
-
-    def channels(g):
-        return pl.ds(g * STEP_CHAN, STEP_CHAN)
-
-    def loads(g):
-        some = channels(g)
-        pairs = [(rows_hbm.at[some], rows_ref.at[some]), (near_hbm.at[some], near_ref.at[some])]
-        pairs += [(far_hbm.at[some], far_ref.at[some]), (crossed_hbm.at[:, some], crossed_ref.at[:, some])]
-        return [pltpu.make_async_copy(a, b, load_sem.at[g, i]) for i, (a, b) in enumerate(pairs)]
+    groups = LOCAL_CHAN // STEP_CHAN
 
     def store(g):
-        return pltpu.make_async_copy(out_ref.at[channels(g)], out_hbm.at[channels(g)], out_sem.at[g])
-
-    groups = LOCAL_CHAN // STEP_CHAN
+        slot = lax.rem(g, SLOTS)
+        return pltpu.make_async_copy(
+            out_ref.at[slot], out_hbm.at[pl.ds(g * STEP_CHAN, STEP_CHAN)], out_sem.at[slot]
+        )
 
     @pl.loop(0, groups)
     def _(g):
-        for copy in loads(g):
-            copy.start()
-
-    @pl.loop(0, groups)
-    def _(g):
-        for copy in loads(g):
-            copy.wait()
+        @pl.when(g >= SLOTS)
+        def _():
+            store(g - SLOTS).wait()
+
+        slot = lax.rem(g, SLOTS)
+        k = g * STEP_CHAN // CHUNK_CHAN
         down_share = lax.rem(g // (FOLD_CHAN // STEP_CHAN), 2)
         near_plane = lax.rem(z + 3 + 2 * down_share, 4)
         far_plane = lax.rem(z + 2, 4)
         crossed_plane = lax.rem(z + 1 + 2 * down_share, 4)
-        for index in range(STEP_CHAN):
-            c = g * STEP_CHAN + index
-            start = pl.multiple_of(xl * 64, 64)
+        for c in range(STEP_CHAN):
+            place = lax.rem(g * STEP_CHAN, CHUNK_CHAN) + c
             parts = []
             for part in range(2):
-                pieces = [rows_ref[c, part, pl.ds(start, 64)], near_ref[c, part], far_ref[c, part]]
-                parts.append(jnp.concatenate(pieces, axis=0))
-            value = lax.dot_general(
-                jnp.concatenate(parts, axis=1), stacked(rows_ref[c, 0], rows_ref[c, 1]), (((1,), (1,)), ((), ())),
+                pieces = [rows[k, 2 * place + part, xl], near[k, 2 * place + part], far[k, 2 * place + part]]
+                parts.append(jnp.concatenate([piece.reshape(64, SPEC) for piece in pieces], axis=0))
+            row_side = [rows[k, 2 * place + part].reshape(128, SPEC) for part in range(2)]
+            both = lax.dot_general(
+                jnp.concatenate(parts, axis=0), jnp.concatenate(row_side, axis=0), (((1,), (1,)), ((), ())),
                 preferred_element_type=F32,
             )
-            value = value * (1.0 / SPEC)
+            value = jnp.concatenate(
+                [both[:192, :128] + both[192:, 128:], both[:192, 128:] - both[192:, :128]], axis=1
+            ) * (1.0 / SPEC)
             for index, plane in enumerate((z, near_plane, far_plane)):
-                out_ref[c, 0, plane] = value[index * 64 : index * 64 + 64, :128]
-                out_ref[c, 1, plane] = value[index * 64 : index * 64 + 64, 128:]
-            sides = [crossed_ref[side, c].astype(F32) for side in range(2)]
-            out_ref[c, 0, crossed_plane] = jnp.concatenate([side[:, :64] for side in sides], axis=1)
-            out_ref[c, 1, crossed_plane] = jnp.concatenate([side[:, 64:] for side in sides], axis=1)
+                out_ref[slot, c, 0, plane] = value[index * 64 : index * 64 + 64, :128]
+                out_ref[slot, c, 1, plane] = value[index * 64 : index * 64 + 64, 128:]
+            sides = [crossed[side, k, place].astype(F32) for side in range(2)]
+            out_ref[slot, c, 0, crossed_plane] = jnp.concatenate([side[:, :64] for side in sides], axis=1)
+            out_ref[slot, c, 1, crossed_plane] = jnp.concatenate([side[:, 64:] for side in sides], axis=1)
         store(g).start()
 
-    @pl.loop(0, groups)
+    @pl.loop(groups - SLOTS, groups)
     def _(g):
         store(g).wait()
 
 
 def correlate(rows, near, far, crossed):
-    any_space = pl.BlockSpec(memory_space=pl.ANY)
-    groups = LOCAL_CHAN // STEP_CHAN
     return pl.pallas_call(
         correlate_kernel,
-        in_specs=[any_space] * 4,
-        out_specs=any_space,
+        in_specs=[pl.BlockSpec(memory_space=pltpu.VMEM)] * 4,
+        out_specs=pl.BlockSpec(memory_space=pl.ANY),
         out_shape=jax.ShapeDtypeStruct((LOCAL_CHAN, 2, 4, 64, 128), F32),
         scratch_shapes=[
-            pltpu.VMEM(rows.shape, BF16),
-            pltpu.VMEM(near.shape, BF16),
-            pltpu.VMEM(far.shape, BF16),
-            pltpu.VMEM(crossed.shape, BF16),
-            pltpu.VMEM((LOCAL_CHAN, 2, 4, 64, 128), F32),
-            pltpu.SemaphoreType.DMA((groups, 4)),
-            pltpu.SemaphoreType.DMA((groups,)),
+            pltpu.VMEM((SLOTS, STEP_CHAN, 2, 4, 64, 128), F32),
+            pltpu.SemaphoreType.DMA((SLOTS,)),
         ],
-        compiler_params=pltpu.CompilerParams(vmem_limit_bytes=58 << 20),
+        compiler_params=pltpu.CompilerParams(vmem_limit_bytes=20 << 20),
         name="correlate",
     )(rows, near, far, crossed)
 
 
 def shards(table, voltages, tap_table):
     rows, near, far, crossed = exchange(jnp.transpose(voltages, (1, 0, 2)), tap_table, table)
-    rows = rows.reshape(LOCAL_CHAN, 2, 128, SPEC)
-    near = near.reshape(LOCAL_CHAN, 2, 64, SPEC)
-    far = far.reshape(LOCAL_CHAN, 2, 64, SPEC)
-    crossed = crossed.reshape(2, LOCAL_CHAN, 64, 128)
     return correlate(rows, near, far, crossed)
 
 

time: 170 us -> 164 us (0.965)
  Pallas kernels: 170 us -> 164 us
    pallas_call x1, Pallas kernels: 13.3 us -> 8.13 us  [correlate(): pl.pallas_call(correlate_kernel, in_specs=[pl.BlockSpec(memory_space=pltp...]
where the time goes in v5:
time: 164 us
  Pallas kernels  164 us (100%)
    pallas_call x1, Pallas kernels, exchange(): pl.pallas_call(exchange_kernel, in_specs=[any_space, pl.BlockSpec(memory_...  156 us
    pallas_call x1, Pallas kernels, correlate(): pl.pallas_call(correlate_kernel, in_specs=[pl.BlockSpec(memory_space=pltp...  8.13 us

profile of v5, /device:TPU:2, one launch (start us, length us, event | category | flops | bytes accessed | tf_op | source)
XLA Modules:
  0.0 164.0 jit_solution(7459523390953100734)
XLA Ops:
  0.0 155.9 %exchange.1 = (bf16[4,32,2,4,2,8,256]{6,5,4,3,2,1,0:T(8,128)(2,1)S(1)}, bf16[4,32,4,2,8,256]{5,4,3,2,1,0:T(8,128)(2,1)S(1)}, bf16[4,32,4,2,8,256]{5,4,3,2,1,0:T(8,128)(2,1)S(1)}, bf16[2,4,16,64,128]{4,3,2,1,0:T(8,128)(2,1)S(1)}) custom-call(bf16[259,4,2048]{2,1,0:T(4,128)(2,1)} %bitcast.1, s32[4,2048]{1,0:T(4,128)} %taps_ref.1, ...), custom_call_target="tpu_custom_call" | custom-call | tf_op jit(solution)/shard_map/exchange/pallas_call | solution.py:341
  155.9 8.1 %correlate.1 = f32[64,2,4,64,128]{4,3,2,1,0:T(8,128)} custom-call(bf16[4,32,2,4,2,8,256]{6,5,4,3,2,1,0:T(8,128)(2,1)S(1)} %get-tuple-element.9.rows, bf16[4,32,4,2,8,256]{5,4,3,2,1,0:T(8,128)(2,1)S(1)} %get-tuple-element.10.near, bf16[4,32,4,2,8,256]{5,4,3,2,1,0:T(8,128)(2,1)S(1)} %get-tuple-element.11.far, ...), custom_call_target="tpu_custom_call" | custom-call | tf_op jit(solution)/shard_map/correlate/pallas_call | solution.py:432

commit v6 on v5

--- a/solution.py
+++ b/solution.py
@@ -82,10 +82,10 @@
                 folded[parity, 1, half, slot // 2, place : place + HALF_SPEC, pl.ds(low, 128)] = rest
 
 
-def transform_chunk(half, quarter, core, table_ref, folded, turned, write):
+def transform_rows(half, quarter, core, table_ref, folded, turned, first_duo, last_duo):
     contract = (((1,), (1,)), ((), ()))
 
-    @pl.loop(0, 4)
+    @pl.loop(first_duo, last_duo)
     def _(duo):
         for parity in range(2):
             top = folded[parity, 0, half, duo]
@@ -101,6 +101,8 @@
                         part * (ROWS // 2) : (part + 1) * (ROWS // 2), sub * 128 : sub * 128 + 128
                     ]
 
+
+def round_rows(turned, write):
     block = CHUNK_CHAN * 16
 
     @pl.loop(0, TARGETS)
@@ -234,44 +236,53 @@
         )
 
     def multiply(k):
-        @pl.loop(0, CHUNK_CHAN)
-        def _(c):
-            left = [rows[k, 2 * c + part].reshape(128, SPEC) for part in range(2)]
-            right = [near[k, 2 * c + part].reshape(64, SPEC) for part in range(2)]
-            value = lax.dot_general(
-                jnp.concatenate(left, axis=1), stacked(right[0], right[1]), (((1,), (1,)), ((), ())),
-                preferred_element_type=F32,
-            )
-            value = (value * (1.0 / SPEC)).astype(BF16)
-            products[k, 0, c] = value[:64]
-            products[k, 1, c] = value[64:]
-
         for way in range(2):
+
+            @pl.loop(way * FOLD_CHAN, (way + 1) * FOLD_CHAN)
+            def _(c):
+                left = [rows[k, 2 * c + part].reshape(128, SPEC) for part in range(2)]
+                right = [near[k, 2 * c + part].reshape(64, SPEC) for part in range(2)]
+                value = lax.dot_general(
+                    jnp.concatenate(left, axis=1), stacked(right[0], right[1]), (((1,), (1,)), ((), ())),
+                    preferred_element_type=F32,
+                )
+                value = (value * (1.0 / SPEC)).astype(BF16)
+                products[k, 0, c] = value[:64]
+                products[k, 1, c] = value[64:]
+
             for side in range(2):
                 back(k, way, side).start()
 
-    def fold(half):
+    def fold_own(half):
         load(half).wait()
         filter_half(half, own, 0, taps_ref, frames, mixed, folded)
+
+    def fold_other(half):
         swap(half).wait_recv()
         filter_half(half, other, 4, taps_ref, frames, mixed, folded)
 
-    fold(0)
-    for quarter in range(CHUNKS):
+    fold_own(0)
+    load_table(0).wait()
+    transform_rows(0, 0, core, table, folded, turned, 0, 2)
+    fold_other(0)
+    for quarter in range(1, CHUNKS):
         load_table(quarter).wait()
 
     @pl.loop(0, STEPS + BACK_LAG)
     def _(turn):
         @pl.when(turn == CHUNKS)
         def _():
-            fold(1)
+            fold_own(1)
+            fold_other(1)
 
         @pl.when(turn < STEPS)
         def _():
             def write(target, value):
                 made[turn, target] = value
 
-            transform_chunk(turn // CHUNKS, lax.rem(turn, CHUNKS), core, table, folded, turned, write)
+            first_duo = 2 - 2 * lax.min(turn, 1)
+            transform_rows(turn // CHUNKS, lax.rem(turn, CHUNKS), core, table, folded, turned, first_duo, 4)
+            round_rows(turned, write)
             local(turn).start()
             for step in range(1, 4):
                 first(turn, step, 0).start()

time: 164 us -> 160 us (0.976)
  Pallas kernels: 164 us -> 160 us
    pallas_call x1, Pallas kernels: 156 us -> 152 us  [exchange(): pl.pallas_call(exchange_kernel, in_specs=[any_space, pl.BlockSpec(memory_...]
where the time goes in v6:
time: 160 us
  Pallas kernels  160 us (100%)
    pallas_call x1, Pallas kernels, exchange(): pl.pallas_call(exchange_kernel, in_specs=[any_space, pl.BlockSpec(memory_...  152 us
    pallas_call x1, Pallas kernels, correlate(): pl.pallas_call(correlate_kernel, in_specs=[pl.BlockSpec(memory_space=pltp...  8.13 us

profile of v6, /device:TPU:2, one launch (start us, length us, event | category | flops | bytes accessed | tf_op | source)
XLA Modules:
  0.0 159.9 jit_solution(17650128592432521852)
XLA Ops:
  0.0 151.7 %exchange.1 = (bf16[4,32,2,4,2,8,256]{6,5,4,3,2,1,0:T(8,128)(2,1)S(1)}, bf16[4,32,4,2,8,256]{5,4,3,2,1,0:T(8,128)(2,1)S(1)}, bf16[4,32,4,2,8,256]{5,4,3,2,1,0:T(8,128)(2,1)S(1)}, bf16[2,4,16,64,128]{4,3,2,1,0:T(8,128)(2,1)S(1)}) custom-call(bf16[259,4,2048]{2,1,0:T(4,128)(2,1)} %bitcast.1, s32[4,2048]{1,0:T(4,128)} %taps_ref.1, ...), custom_call_target="tpu_custom_call" | custom-call | tf_op jit(solution)/shard_map/exchange/pallas_call | solution.py:352
  151.7 8.1 %correlate.1 = f32[64,2,4,64,128]{4,3,2,1,0:T(8,128)} custom-call(bf16[4,32,2,4,2,8,256]{6,5,4,3,2,1,0:T(8,128)(2,1)S(1)} %get-tuple-element.9.rows, bf16[4,32,4,2,8,256]{5,4,3,2,1,0:T(8,128)(2,1)S(1)} %get-tuple-element.10.near, bf16[4,32,4,2,8,256]{5,4,3,2,1,0:T(8,128)(2,1)S(1)} %get-tuple-element.11.far, ...), custom_call_target="tpu_custom_call" | custom-call | tf_op jit(solution)/shard_map/correlate/pallas_call | solution.py:443

commit v7 on v6

--- a/solution.py
+++ b/solution.py
@@ -23,8 +23,8 @@
 ROWS = 2 * TARGETS * FOLD_CHAN
 HALF_SPEC = SPEC // 2
 STEPS = 2 * CHUNKS
-STEP_CHAN = 4
-SLOTS = 6
+STEP_CHAN = 8
+SLOTS = 3
 PAIR_LAG = 2
 PASS_LAG = 3
 BACK_LAG = 4
@@ -300,7 +300,6 @@
             for step in range(4):
                 first_arrival(t, step, 1).wait_recv()
             pair(t, 1).start()
-            pair(t, 0).start()
 
         @pl.when((turn >= PAIR_LAG) & (turn < STEPS + PAIR_LAG))
         def _():
@@ -317,6 +316,10 @@
                     ring(t, part, way).wait_recv()
                     onward(t, part, way).start()
             pair(t, 0, False).wait_recv()
+
+        @pl.when((turn >= 1) & (turn <= STEPS))
+        def _():
+            pair(turn - 1, 0).start()
 
         @pl.when(turn >= CHUNKS + BACK_LAG)
         def _():

time: 160 us -> 159 us (level)
  no operation moved by 1% of the time
where the time goes in v7:
time: 159 us
  Pallas kernels  159 us (100%)
    pallas_call x1, Pallas kernels, exchange(): pl.pallas_call(exchange_kernel, in_specs=[any_space, pl.BlockSpec(memory_...  152 us
    pallas_call x1, Pallas kernels, correlate(): pl.pallas_call(correlate_kernel, in_specs=[pl.BlockSpec(memory_space=pltp...  7.15 us

profile of v7, /device:TPU:2, one launch (start us, length us, event | category | flops | bytes accessed | tf_op | source)
XLA Modules:
  0.0 158.9 jit_solution(10483392601898544352)
XLA Ops:
  0.0 151.7 %exchange.1 = (bf16[4,32,2,4,2,8,256]{6,5,4,3,2,1,0:T(8,128)(2,1)S(1)}, bf16[4,32,4,2,8,256]{5,4,3,2,1,0:T(8,128)(2,1)S(1)}, bf16[4,32,4,2,8,256]{5,4,3,2,1,0:T(8,128)(2,1)S(1)}, bf16[2,4,16,64,128]{4,3,2,1,0:T(8,128)(2,1)S(1)}) custom-call(bf16[259,4,2048]{2,1,0:T(4,128)(2,1)} %bitcast.1, s32[4,2048]{1,0:T(4,128)} %taps_ref.1, ...), custom_call_target="tpu_custom_call" | custom-call | tf_op jit(solution)/shard_map/exchange/pallas_call | solution.py:355
  151.7 7.1 %correlate.1 = f32[64,2,4,64,128]{4,3,2,1,0:T(8,128)} custom-call(bf16[4,32,2,4,2,8,256]{6,5,4,3,2,1,0:T(8,128)(2,1)S(1)} %get-tuple-element.9.rows, bf16[4,32,4,2,8,256]{5,4,3,2,1,0:T(8,128)(2,1)S(1)} %get-tuple-element.10.near, bf16[4,32,4,2,8,256]{5,4,3,2,1,0:T(8,128)(2,1)S(1)} %get-tuple-element.11.far, ...), custom_call_target="tpu_custom_call" | custom-call | tf_op jit(solution)/shard_map/correlate/pallas_call | solution.py:446

commit v8 on v7

--- a/solution.py
+++ b/solution.py
@@ -111,10 +111,6 @@
         write(target, rows.reshape(2 * CHUNK_CHAN, 8, 128).astype(BF16))
 
 
-def stacked(real, imag):
-    return jnp.concatenate([jnp.concatenate([real, imag], axis=1), jnp.concatenate([imag, -real], axis=1)], axis=0)
-
-
 def exchange_kernel(
     own_ref, taps_ref, table_hbm, rows, near, far, crossed,
     own, other, table, frames, mixed, folded, turned, made, products,
@@ -242,11 +238,13 @@
             def _(c):
                 left = [rows[k, 2 * c + part].reshape(128, SPEC) for part in range(2)]
                 right = [near[k, 2 * c + part].reshape(64, SPEC) for part in range(2)]
-                value = lax.dot_general(
-                    jnp.concatenate(left, axis=1), stacked(right[0], right[1]), (((1,), (1,)), ((), ())),
+                both = lax.dot_general(
+                    jnp.concatenate(left, axis=0), jnp.concatenate(right, axis=0), (((1,), (1,)), ((), ())),
                     preferred_element_type=F32,
                 )
-                value = (value * (1.0 / SPEC)).astype(BF16)
+                real = both[:128, :64] + both[128:, 64:]
+                imag = both[:128, 64:] - both[128:, :64]
+                value = (jnp.concatenate([real, imag], axis=1) * (1.0 / SPEC)).astype(BF16)
                 products[k, 0, c] = value[:64]
                 products[k, 1, c] = value[64:]
 

time: 159 us -> 159 us (level)
  no operation moved by 1% of the time
where the time goes in v8:
time: 159 us
  Pallas kernels  159 us (100%)
    pallas_call x1, Pallas kernels, exchange(): pl.pallas_call(exchange_kernel, in_specs=[any_space, pl.BlockSpec(memory_...  152 us
    pallas_call x1, Pallas kernels, correlate(): pl.pallas_call(correlate_kernel, in_specs=[pl.BlockSpec(memory_space=pltp...  7.15 us

profile of v8, /device:TPU:2, one launch (start us, length us, event | category | flops | bytes accessed | tf_op | source)
XLA Modules:
  0.0 158.9 jit_solution(12494085183367482975)
XLA Ops:
  0.0 151.7 %exchange.1 = (bf16[4,32,2,4,2,8,256]{6,5,4,3,2,1,0:T(8,128)(2,1)S(1)}, bf16[4,32,4,2,8,256]{5,4,3,2,1,0:T(8,128)(2,1)S(1)}, bf16[4,32,4,2,8,256]{5,4,3,2,1,0:T(8,128)(2,1)S(1)}, bf16[2,4,16,64,128]{4,3,2,1,0:T(8,128)(2,1)S(1)}) custom-call(bf16[259,4,2048]{2,1,0:T(4,128)(2,1)} %bitcast.1, s32[4,2048]{1,0:T(4,128)} %taps_ref.1, ...), custom_call_target="tpu_custom_call" | custom-call | tf_op jit(solution)/shard_map/exchange/pallas_call | solution.py:353
  151.7 7.1 %correlate.1 = f32[64,2,4,64,128]{4,3,2,1,0:T(8,128)} custom-call(bf16[4,32,2,4,2,8,256]{6,5,4,3,2,1,0:T(8,128)(2,1)S(1)} %get-tuple-element.9.rows, bf16[4,32,4,2,8,256]{5,4,3,2,1,0:T(8,128)(2,1)S(1)} %get-tuple-element.10.near, bf16[4,32,4,2,8,256]{5,4,3,2,1,0:T(8,128)(2,1)S(1)} %get-tuple-element.11.far, ...), custom_call_target="tpu_custom_call" | custom-call | tf_op jit(solution)/shard_map/correlate/pallas_call | solution.py:444
